TPU v7x, 32 devices: a whole 2x2x4 slice. The times are simulated.
32 devices in a mesh: cuts: 4 (over z), tile: 8 (over y, x, core).
Axes of the slice: x: 2, y: 2, z: 4, core: 2. Of those that a mesh axis runs over, the one named last changes fastest.
Arguments:
- start_states: float32 [4, 3, 128, 2048], P('cuts', None, 'tile'), may hold values from -6 to 6
Outputs:
- next_states: float32 [4, 3, 128, 2048], P('cuts', None, 'tile')
All inputs are finite; a program needn't handle non-finite values.
Results may differ from a plain program's by a relative error of at most 0.0001.
Values sent between devices are 32-bit elements; how exact they have to be, the bound alone decides.
A program may use at most 128 MiB of HBM per device.

v0:
```python
import functools

import numpy as np
import jax
import jax.numpy as jnp
from jax import lax
from jax.experimental import pallas as pl
from jax.experimental.pallas import tpu as pltpu
from jax.sharding import PartitionSpec as P

STEPS = 3
FINE_SPACING = 0.05
COARSE_SPACING = 0.1
FINE_STEP = 0.015
COARSE_STEP = 0.045
LANES = 128
SUB = 8
HALO = (2, 2, 3)
MESH = pl.DeviceIdType.MESH
HIGH = lax.Precision.HIGH


def line_tables(tiles, fine_tiles, stride, length, spacing, step):
    groups = LANES // fine_tiles
    lane = np.arange(LANES)
    chunk = (lane % fine_tiles) * groups + lane // fine_tiles
    columns = tiles * LANES
    centers = (np.arange(columns) + 0.5) * stride
    depth = (0.9 + 0.3 * np.sin(6.0 * np.pi * centers / length)).reshape(LANES, tiles).T
    beta = depth * depth / 3.0
    b = beta / spacing**2
    mid = 1.0 + 2.0 * b
    last = tiles - 1
    inv = np.zeros_like(b)
    cp = np.zeros_like(b)
    for j in range(last):
        inv[j] = 1.0 / (mid[j] - (b[j] * cp[j - 1] if j else 0.0))
        cp[j] = b[j] * inv[j]
    run = np.ones_like(b)
    for j in range(1, tiles):
        run[j] = run[j - 1] * cp[j - 1]
    p = np.zeros_like(b)
    q = np.zeros_like(b)
    q[last] = 1.0
    for j in range(last - 1, -1, -1):
        p[j] = run[j + 1] + cp[j] * p[j + 1]
        q[j] = cp[j] * q[j + 1]
    system = np.zeros((LANES, LANES))
    for k in range(LANES):
        system[k, k] = mid[last, k] - b[last, k] * q[last - 1, k]
        if k:
            system[k, k - 1] = -b[last, k] * p[last - 1, k]
        if k + 1 < LANES:
            system[k, k] -= b[last, k] * p[0, k + 1]
            system[k, k + 1] = -b[last, k] * q[0, k + 1]
    solve = np.linalg.inv(system).T
    weights = np.zeros((2 * LANES, 2 * LANES))
    weights[:LANES, :LANES] = solve
    weights[LANES + 1 :, :LANES] = solve[:-1] * b[last, :-1, None]
    weights[:, LANES + 1 :] = weights[:, : LANES - 1]
    both = np.concatenate([chunk, LANES + chunk])
    weights = weights[both][:, both]
    slope = step * depth / (2.0 * spacing)
    weight = beta / (spacing**2 + 4.0 * beta)
    inv[last] = b[last]
    rows = np.stack([inv, cp, run, slope, weight])[:, :, chunk]
    return rows.astype(np.float32), weights.astype(np.float32)


def relaid(tiles):
    tiles = list(tiles)
    lane = lax.broadcasted_iota(jnp.int32, tiles[0].shape, 1)
    bit = 1
    while bit < len(tiles):
        keep = (lane & bit) == 0
        for t in range(len(tiles)):
            if t & bit == 0:
                a, b = tiles[t], tiles[t | bit]
                tiles[t] = jnp.where(keep, a, pltpu.roll(b, bit, 1))
                tiles[t | bit] = jnp.where(keep, pltpu.roll(a, LANES - bit, 1), b)
        bit *= 2
    return tiles


def wave(state, height, held, rows, weights, tiles, fine_tiles, factor, inside):
    count = state.shape[2]
    lane = lax.broadcasted_iota(jnp.int32, (count, LANES), 1)

    def chunk_before(x):
        wrapped = jnp.where(lane == 0, 0.0, pltpu.roll(x, fine_tiles + 1, 1))
        return jnp.where(lane >= fine_tiles, pltpu.roll(x, fine_tiles, 1), wrapped)

    def chunk_after(x):
        wrapped = jnp.where(lane == LANES - 1, 0.0, pltpu.roll(x, LANES - fine_tiles - 1, 1))
        return jnp.where(lane < LANES - fine_tiles, pltpu.roll(x, LANES - fine_tiles, 1), wrapped)

    def below(x):
        return pltpu.roll(x, count - 1, 0)

    def above(x):
        return pltpu.roll(x, 1, 0)

    def across(load, j):
        right = load(j + 1) if j + 1 < tiles else chunk_after(load(0))
        left = load(j - 1) if j else chunk_before(load(tiles - 1))
        return right - left

    def table(kind, j):
        return rows[kind, pl.ds(j, 1), :]

    for j in range(tiles):
        flux_y = state[2, j]
        spread = across(lambda i: state[1, i], j) + (below(flux_y) - above(flux_y))
        height[j] = (state[0, j] - factor * spread) * inside
    total = None
    inner = None
    for j in range(tiles):
        middle = height[j]
        slope = table(3, j)
        force_x = state[1, j] - slope * across(lambda i: height[i], j)
        force_y = state[2, j] - slope * (below(middle) - above(middle))
        force = jnp.concatenate([force_x, force_y], axis=0)
        if j == tiles - 1:
            edge = force + table(0, j) * inner
        elif j == 0:
            inner = force * table(0, j)
            total = inner
            held[j] = inner
        else:
            inner = force * table(0, j) + table(1, j) * inner
            total = total + table(2, j) * inner
            held[j] = inner
    met = jnp.dot(
        jnp.concatenate([edge, total], axis=1),
        weights[...],
        precision=HIGH,
        preferred_element_type=jnp.float32,
    )
    value = met[:, :LANES]
    before = met[:, LANES:]
    for j in range(tiles - 1, -1, -1):
        if j < tiles - 1:
            value = held[j] + table(2, j + 1) * before + table(1, j) * value
        weight = table(4, j)
        for part in range(2):
            trial = value[part * count : (part + 1) * count] * inside
            change = trial - state[1 + part, j]
            curve = below(change) - 2.0 * change + above(change)
            state[1 + part, j] = (trial + weight * curve) * inside
        state[0, j] = height[j]


def kernel(
    tile_count, slices, x_hbm, fine_rows_hbm, fine_weights_hbm, coarse_rows_hbm,
    coarse_weights_hbm, fine_hbm, gain_ref,
    natural, x_ref, fine_rows, fine_weights, coarse_rows, coarse_weights,
    up_main, down_main, edge, up_edge, down_edge, state, height, held,
    c_state, c_height, c_held, start, end, arrived, leaving, low, far_start, above_in, below_in,
    local, send, recv,
):
    cut = lax.axis_index("cuts")
    tile = lax.axis_index("tile")
    has_up = tile > 0
    has_down = tile < tile_count - 1
    has_before = cut > 0
    has_after = cut < slices - 1
    planes, row_count, columns = x_ref.shape
    tiles = columns // LANES
    half = tiles // 2
    groups = row_count // SUB
    total_rows = row_count * tile_count
    coarse_count = row_count // 2

    pairs = [
        (x_hbm, x_ref), (fine_rows_hbm, fine_rows), (fine_weights_hbm, fine_weights),
        (coarse_rows_hbm, coarse_rows), (coarse_weights_hbm, coarse_weights),
    ]
    loads = [pltpu.make_async_copy(a, b, local.at[i]) for i, (a, b) in enumerate(pairs)]
    for load in loads:
        load.start()

    barrier = pltpu.get_barrier_semaphore()
    near = [(has_up, cut, tile - 1), (has_down, cut, tile + 1)]
    for there, other in ((has_before, cut - 1), (has_after, cut + 1)):
        near.append((there, other, tile))
        near.append((there & has_up, other, tile - 1))
        near.append((there & has_down, other, tile + 1))
    for exists, to_cut, to_tile in near:
        @pl.when(exists)
        def _():
            pl.semaphore_signal(
                barrier, inc=1, device_id=(to_cut, to_tile), device_id_type=MESH
            )
    pl.semaphore_wait(barrier, sum(exists.astype(jnp.int32) for exists, _, _ in near))

    def remote(source, target, which, to_cut, to_tile):
        return pltpu.make_async_remote_copy(
            src_ref=source, dst_ref=target, send_sem=send.at[which], recv_sem=recv.at[which],
            device_id=(to_cut, to_tile), device_id_type=MESH,
        )

    one = pl.ds(0, 1)
    main_down = remote(
        x_hbm.at[:, pl.ds(row_count - SUB, SUB)], up_main, 0, cut, tile + 1
    )
    edge_down = remote(edge.at[one], up_edge.at[one], 1, cut, tile + 1)
    main_up = remote(x_hbm.at[:, pl.ds(0, SUB)], down_main, 2, cut, tile - 1)
    edge_up = remote(x_hbm.at[planes - 1, pl.ds(SUB, 1)], down_edge.at[one], 3, cut, tile - 1)

    @pl.when(has_down)
    def _():
        main_down.start()

    @pl.when(has_up)
    def _():
        edge_up.start()
        main_up.start()

    loads[0].wait()
    edge[one, :] = x_ref[planes - 1, pl.ds(row_count - SUB - 1, 1), :]

    def place_rows(values, plane, row):
        parts = relaid([values[:, t * LANES : (t + 1) * LANES] for t in range(tiles)])
        for j in range(tiles):
            state[plane, j, pl.ds(row, SUB), :] = parts[j]

    tail = SUB * (groups + 2)
    for plane in range(planes - 1):
        for group in range(groups):
            place_rows(x_ref[plane, pl.ds(group * SUB, SUB), :], plane, SUB * (group + 1))
        for j in range(tiles):
            state[plane, j, pl.ds(tail, SUB), :] = jnp.zeros((SUB, LANES), jnp.float32)

    @pl.when(has_down)
    def _():
        edge_down.start()

    for group in range(groups):
        place_rows(
            x_ref[planes - 1, pl.ds(group * SUB, SUB), :], planes - 1, SUB * (group + 1)
        )

    def restricted(plane, j, row, count):
        parts = [
            state[plane, 2 * j + k, pl.ds(row + r, count, stride=2), :]
            for r in range(2)
            for k in range(2)
        ]
        return 0.25 * ((parts[0] + parts[1]) + (parts[2] + parts[3]))

    def each_slab():
        return [(plane, j) for plane in range(planes) for j in range(half)]

    for plane, j in each_slab():
        start[plane, j] = restricted(plane, j, SUB, coarse_count)
    for load in loads[1:]:
        load.wait()

    @pl.when(jnp.logical_not(has_up))
    def _():
        up_main[...] = jnp.zeros_like(up_main)
        up_edge[...] = jnp.zeros_like(up_edge)

    @pl.when(jnp.logical_not(has_down))
    def _():
        down_main[...] = jnp.zeros_like(down_main)
        down_edge[...] = jnp.zeros_like(down_edge)

    @pl.when(has_up)
    def _():
        main_down.wait_recv()
        edge_down.wait_recv()

    @pl.when(has_down)
    def _():
        main_up.wait_recv()
        edge_up.wait_recv()

    for plane in range(planes):
        place_rows(up_main[plane], plane, 0)
        place_rows(down_main[plane], plane, tail - SUB)
    at_row = lax.broadcasted_iota(jnp.int32, (SUB, columns), 0)
    mixed = jnp.where(
        at_row == 0,
        jnp.broadcast_to(down_edge[one, :], (SUB, columns)),
        jnp.where(
            at_row == SUB - 1, jnp.broadcast_to(up_edge[one, :], (SUB, columns)), 0.0
        ),
    )
    place_rows(mixed, planes - 1, tail)

    for plane, j in each_slab():
        far_start[plane, j, pl.ds(0, SUB // 2), :] = restricted(plane, j, tail - SUB, SUB // 2)
        far_start[plane, j, pl.ds(SUB // 2, SUB // 2), :] = restricted(plane, j, 0, SUB // 2)

    def mask(count, lead, total, origin):
        at = lax.broadcasted_iota(jnp.int32, (count, LANES), 0)
        row = jnp.where(at >= count - SUB // 2, at - count, at) - lead + origin
        return ((row >= 0) & (row < total)).astype(jnp.float32)

    fine_inside = mask(tail + SUB, SUB, total_rows, tile * row_count)

    def fine_step(step, carry):
        wave(
            state, height, held, fine_rows, fine_weights, tiles, tiles,
            FINE_STEP / (2.0 * FINE_SPACING), fine_inside,
        )
        return carry

    lax.fori_loop(0, STEPS, fine_step, 0)

    last = planes - 1
    first_part = (pl.ds(0, last), slice(None), pl.ds(0, HALO[0]))
    last_part = (last, slice(None), pl.ds(0, HALO[last]))
    to_own = remote(leaving, arrived, 4, cut + 1, tile)
    to_above = [
        remote(leaving.at[part], below_in.at[part], 5 + i, cut + 1, tile - 1)
        for i, part in enumerate((first_part, last_part))
    ]
    to_below = [
        remote(low.at[part], above_in.at[part], 7 + i, cut + 1, tile + 1)
        for i, part in enumerate((first_part, last_part))
    ]

    def leave(plane, j, value):
        leaving[plane, j] = value
        low[plane, j] = pltpu.roll(value, HALO[plane], 0)

    def launch():
        @pl.when(has_after & has_up)
        def _():
            for copy in to_above:
                copy.start()

        @pl.when(has_after & has_down)
        def _():
            for copy in to_below:
                copy.start()

        @pl.when(has_after)
        def _():
            to_own.start()

    @pl.when(cut == 0)
    def _():
        for plane, j in each_slab():
            leave(plane, j, restricted(plane, j, SUB, coarse_count))
        launch()
        gain_ref[...] = jnp.zeros_like(gain_ref)

    for plane in range(planes):
        for group in range(groups):
            rows = pl.ds(SUB * (group + 1), SUB)
            parts = relaid([state[plane, j, rows, :] for j in range(tiles)])
            for t in range(tiles):
                natural[plane, pl.ds(group * SUB, SUB), pl.ds(t * LANES, LANES)] = parts[t]
    store = pltpu.make_async_copy(natural, fine_hbm, local.at[5])
    store.start()

    @pl.when(has_before)
    def _():
        for plane, j in each_slab():
            end[plane, j] = restricted(plane, j, SUB, coarse_count)

        @pl.when(jnp.logical_not(has_up))
        def _():
            above_in[...] = jnp.zeros_like(above_in)

        @pl.when(jnp.logical_not(has_down))
        def _():
            below_in[...] = jnp.zeros_like(below_in)

        @pl.when(has_up)
        def _():
            for copy in to_below:
                copy.wait_recv()

        @pl.when(has_down)
        def _():
            for copy in to_above:
                copy.wait_recv()

        at = lax.broadcasted_iota(jnp.int32, (SUB, LANES), 0)
        for plane, j in each_slab():
            around = jnp.where(
                at < HALO[plane],
                below_in[plane, j],
                jnp.where(
                    at >= SUB - HALO[plane],
                    pltpu.roll(above_in[plane, j], SUB - HALO[plane], 0),
                    0.0,
                ),
            )
            c_state[plane, j, pl.ds(coarse_count, SUB), :] = around - far_start[plane, j]
        to_own.wait_recv()
        for plane, j in each_slab():
            c_state[plane, j, pl.ds(0, coarse_count), :] = arrived[plane, j] - start[plane, j]
        coarse_inside = mask(coarse_count + SUB, 0, total_rows // 2, tile * coarse_count)
        wave(
            c_state, c_height, c_held, coarse_rows, coarse_weights, half, tiles,
            COARSE_STEP / (2.0 * COARSE_SPACING), coarse_inside,
        )
        for plane, j in each_slab():
            leave(plane, j, c_state[plane, j, pl.ds(0, coarse_count), :] + end[plane, j])
        launch()
        for plane, j in each_slab():
            gain_ref[plane, j] = c_state[plane, j, pl.ds(0, coarse_count), :]

    store.wait()

    @pl.when(has_down)
    def _():
        main_down.wait_send()
        edge_down.wait_send()

    @pl.when(has_up)
    def _():
        main_up.wait_send()
        edge_up.wait_send()

    @pl.when(has_after & has_up)
    def _():
        for copy in to_above:
            copy.wait_send()

    @pl.when(has_after & has_down)
    def _():
        for copy in to_below:
            copy.wait_send()

    @pl.when(has_after)
    def _():
        to_own.wait_send()


def finish(fine_ref, gain_ref, out_hbm, spread, result, done):
    planes, tiles, row_count, _ = spread.shape
    stores = []
    for plane in range(planes):
        parts = relaid([gain_ref[plane, j // 2] for j in range(tiles)])
        for t in range(tiles):
            for r in range(2):
                spread[plane, t, pl.ds(r, row_count // 2, stride=2), :] = parts[t]
        for t in range(tiles):
            columns = pl.ds(t * LANES, LANES)
            result[plane, :, columns] = fine_ref[plane, :, columns] + spread[plane, t]
        stores.append(
            pltpu.make_async_copy(result.at[plane], out_hbm.at[plane], done.at[plane])
        )
        stores[-1].start()
    for store in stores:
        store.wait()


def per_device(tile_count, slices, start_states):
    fields = start_states[0]
    planes, row_count, columns = fields.shape
    tiles = columns // LANES
    half = tiles // 2
    fine = line_tables(tiles, tiles, 1.0, columns, FINE_SPACING, FINE_STEP)
    coarse = line_tables(half, tiles, 2.0, columns, COARSE_SPACING, COARSE_STEP)
    fine_count = row_count + 3 * SUB
    coarse_count = row_count // 2
    f32 = jnp.float32
    slab = pltpu.VMEM((planes, half, coarse_count, LANES), f32)
    fine_end, gain = pl.pallas_call(
        functools.partial(kernel, tile_count, slices),
        out_shape=[
            jax.ShapeDtypeStruct(fields.shape, f32),
            jax.ShapeDtypeStruct((planes, half, coarse_count, LANES), f32),
        ],
        in_specs=[pl.BlockSpec(memory_space=pl.ANY)] * 5,
        out_specs=[
            pl.BlockSpec(memory_space=pl.ANY),
            pl.BlockSpec(memory_space=pltpu.VMEM),
        ],
        scratch_shapes=[pltpu.VMEM(fields.shape, f32)] * 2
        + [pltpu.VMEM(a.shape, f32) for a in fine + coarse]
        + [pltpu.VMEM((planes, SUB, columns), f32)] * 2
        + [pltpu.VMEM((SUB, columns), f32)] * 3
        + [
            pltpu.VMEM((planes, tiles, fine_count, LANES), f32),
            pltpu.VMEM((tiles, fine_count, LANES), f32),
            pltpu.VMEM((tiles, 2 * fine_count, LANES), f32),
            pltpu.VMEM((planes, half, 2 * coarse_count, LANES), f32),
            pltpu.VMEM((half, 2 * coarse_count, LANES), f32),
            pltpu.VMEM((half, 4 * coarse_count, LANES), f32),
        ]
        + [slab] * 8
        + [
            pltpu.SemaphoreType.DMA((6,)),
            pltpu.SemaphoreType.DMA((9,)),
            pltpu.SemaphoreType.DMA((9,)),
        ],
        compiler_params=pltpu.CompilerParams(collective_id=0, has_side_effects=True),
    )(fields, *[jnp.asarray(a) for a in fine + coarse])
    out = pl.pallas_call(
        finish,
        out_shape=jax.ShapeDtypeStruct(fields.shape, f32),
        in_specs=[pl.BlockSpec(memory_space=pltpu.VMEM)] * 2,
        out_specs=pl.BlockSpec(memory_space=pl.ANY),
        scratch_shapes=[
            pltpu.VMEM((planes, tiles, row_count, LANES), f32),
            pltpu.VMEM(fields.shape, f32),
            pltpu.SemaphoreType.DMA((planes,)),
        ],
    )(fine_end, gain)
    return out[None]


def solution(mesh):
    spec = P("cuts", None, "tile", None)
    body = functools.partial(per_device, mesh.shape["tile"], mesh.shape["cuts"])
    return jax.shard_map(body, mesh=mesh, in_specs=(spec,), out_specs=spec, check_vma=False)
```

profile of v0, /device:TPU:27, one launch (start us, length us, event | category | flops | bytes accessed | tf_op | source)
XLA Modules:
  0.0 29.0 jit_solution(12379519988279033997)
XLA Ops:
  0.0 26.9 %shard_map.55 = (f32[3,16,2048]{2,1,0:T(8,128)}, f32[3,8,8,128]{3,2,1,0:T(8,128)}) custom-call(f32[3,16,2048]{2,1,0:T(8,128)} %bitcast.2, f32[5,16,128]{2,1,0:T(8,128)} %constant.8.clone.fine_rows_hbm, f32[256,256]{1,0:T(8,128)} %constant.9.clone.fine_weights_hbm, f32[5,8,128]{2,1,0:T(8,128)} %constant.10.clone.coarse_rows_hbm, ...), custom_call_target="tpu_custom_call" | custom-call | tf_op jit(solution)/shard_map/pallas_call | solution.py:466
  26.9 2.1 %shard_map.56 = f32[3,16,2048]{2,1,0:T(8,128)} custom-call(f32[3,16,2048]{2,1,0:T(8,128)} %get-tuple-element.7.fine_ref, f32[3,8,8,128]{3,2,1,0:T(8,128)} %get-tuple-element.8.gain_ref), custom_call_target="tpu_custom_call" | custom-call | tf_op jit(solution)/shard_map/pallas_call | solution.py:497
where the time goes:
time: 29.2 us; the launch traced here: 29 us
  Pallas kernels  29 us (99%)
    pallas_call x1, Pallas kernels, per_device(): pl.pallas_call(functools.partial(kernel, tile_count, slices), out_shape=[...  26.9 us
    pallas_call x1, Pallas kernels, per_device(): pl.pallas_call(finish, out_shape=jax.ShapeDtypeStruct(fields.shape, f32),...  2.1 us

commit v1 on v0

v1 whole, which is shorter than its diff:
```python
import functools

import ml_dtypes
import numpy as np
import jax
import jax.numpy as jnp
from jax import lax
from jax.experimental import pallas as pl
from jax.experimental.pallas import tpu as pltpu
from jax.sharding import PartitionSpec as P

STEPS = 3
FINE_SPACING = 0.05
COARSE_SPACING = 0.1
FINE_STEP = 0.015
COARSE_STEP = 0.045
LANES = 128
SUB = 8
HALO = (2, 2, 3)
OWN = 2 * SUB
MESH = pl.DeviceIdType.MESH


def line_tables(tiles, fine_tiles, stride, length, spacing, step):
    groups = LANES // fine_tiles
    lane = np.arange(LANES)
    chunk = (lane % fine_tiles) * groups + lane // fine_tiles
    columns = tiles * LANES
    centers = (np.arange(columns) + 0.5) * stride
    depth = (0.9 + 0.3 * np.sin(6.0 * np.pi * centers / length)).reshape(LANES, tiles).T
    beta = depth * depth / 3.0
    b = beta / spacing**2
    mid = 1.0 + 2.0 * b
    last = tiles - 1
    inv = np.zeros_like(b)
    cp = np.zeros_like(b)
    for j in range(last):
        inv[j] = 1.0 / (mid[j] - (b[j] * cp[j - 1] if j else 0.0))
        cp[j] = b[j] * inv[j]
    run = np.ones_like(b)
    for j in range(1, tiles):
        run[j] = run[j - 1] * cp[j - 1]
    p = np.zeros_like(b)
    q = np.zeros_like(b)
    q[last] = 1.0
    for j in range(last - 1, -1, -1):
        p[j] = run[j + 1] + cp[j] * p[j + 1]
        q[j] = cp[j] * q[j + 1]
    system = np.zeros((LANES, LANES))
    for k in range(LANES):
        system[k, k] = mid[last, k] - b[last, k] * q[last - 1, k]
        if k:
            system[k, k - 1] = -b[last, k] * p[last - 1, k]
        if k + 1 < LANES:
            system[k, k] -= b[last, k] * p[0, k + 1]
            system[k, k + 1] = -b[last, k] * q[0, k + 1]
    solve = np.linalg.inv(system).T[chunk][:, chunk]
    high = solve.astype(ml_dtypes.bfloat16)
    low = (solve - high.astype(np.float64)).astype(ml_dtypes.bfloat16)
    half = np.concatenate([high, low], axis=1)
    weights = np.concatenate([half, half], axis=0)
    slope = step * depth / (2.0 * spacing)
    weight = beta / (spacing**2 + 4.0 * beta)
    inv[last] = b[last]
    rows = np.stack([inv, cp, run, slope, weight])[:, :, chunk]
    return rows.astype(np.float32), weights


def relaid(tiles):
    tiles = list(tiles)
    lane = lax.broadcasted_iota(jnp.int32, tiles[0].shape, 1)
    bit = 1
    while bit < len(tiles):
        keep = (lane & bit) == 0
        for t in range(len(tiles)):
            if t & bit == 0:
                a, b = tiles[t], tiles[t | bit]
                tiles[t] = jnp.where(keep, a, pltpu.roll(b, bit, 1))
                tiles[t | bit] = jnp.where(keep, pltpu.roll(a, LANES - bit, 1), b)
        bit *= 2
    return tiles


def wave(state, held, change, rows, weights, inside, tiles, fine_tiles, wide, core):
    factor_in, slope_in, weight_in = inside
    h0, hn = wide
    t0, tn = core
    at = pl.ds(t0, tn)

    def lane(x):
        return lax.broadcasted_iota(jnp.int32, x.shape, 1)

    def chunk_before(x):
        wrapped = jnp.where(lane(x) == 0, 0.0, pltpu.roll(x, fine_tiles + 1, 1))
        return jnp.where(lane(x) >= fine_tiles, pltpu.roll(x, fine_tiles, 1), wrapped)

    def chunk_after(x):
        wrapped = jnp.where(lane(x) == LANES - 1, 0.0, pltpu.roll(x, LANES - fine_tiles - 1, 1))
        return jnp.where(
            lane(x) < LANES - fine_tiles, pltpu.roll(x, LANES - fine_tiles, 1), wrapped
        )

    def across(load, j):
        right = load(j + 1) if j + 1 < tiles else chunk_after(load(0))
        left = load(j - 1) if j else chunk_before(load(tiles - 1))
        return right - left

    def table(kind, j):
        return rows[kind, pl.ds(j, 1), :]

    last = tiles - 1
    near = pl.ds(h0, hn)
    factor = factor_in[near, :]
    for j in range(tiles):
        along = across(lambda i: state[1, i, near, :], j)
        down = state[2, j, pl.ds(h0 + 1, hn), :] - state[2, j, pl.ds(h0 - 1, hn), :]
        state[0, j, near, :] = state[0, j, near, :] - factor * (along + down)
    total = None
    inner = None
    for j in range(tiles):
        along = across(lambda i: state[0, i, at, :], j)
        down = state[0, j, pl.ds(t0 + 1, tn), :] - state[0, j, pl.ds(t0 - 1, tn), :]
        force_x = state[1, j, at, :] - table(3, j) * along
        force_y = state[2, j, at, :] - slope_in[j, at, :] * down
        force = jnp.concatenate([force_x, force_y], axis=0)
        if j == last:
            edge = force + table(0, j) * inner
        elif j == 0:
            inner = force * table(0, j)
            total = inner
            held[j, pl.ds(0, 2 * tn), :] = inner
        else:
            inner = force * table(0, j) + table(1, j) * inner
            total = total + table(2, j) * inner
            held[j, pl.ds(0, 2 * tn), :] = inner
    met = edge + table(0, last) * chunk_after(total)
    high = met.astype(jnp.bfloat16)
    low = (met - high.astype(jnp.float32)).astype(jnp.bfloat16)
    met = jnp.dot(
        jnp.concatenate([high, low], axis=1),
        weights[...],
        preferred_element_type=jnp.float32,
    )
    value = met[:, :LANES] + met[:, LANES:]
    before = chunk_before(value)
    for j in range(last, -1, -1):
        if j < last:
            value = (
                held[j, pl.ds(0, 2 * tn), :] + table(2, j + 1) * before + table(1, j) * value
            )
        for part in range(2):
            trial = value[part * tn : (part + 1) * tn]
            moved = trial - state[1 + part, j, at, :]
            change[j, part, at, :] = moved
            around = change[j, part, pl.ds(t0 + 1, tn), :] + change[j, part, pl.ds(t0 - 1, tn), :]
            state[1 + part, j, at, :] = trial + weight_in[j, at, :] * (around - 2.0 * moved)


def kernel(
    tile_count, slices, x_hbm, fine_rows_hbm, fine_weights_hbm, coarse_rows_hbm,
    coarse_weights_hbm, out_ref,
    x_ref, fine_rows, fine_weights, coarse_rows, coarse_weights,
    down_edge, up_edge, from_up, from_down, state, held, change,
    c_state, c_held, c_change, factor_in, slope_in, weight_in, c_factor_in, c_slope_in,
    c_weight_in, spread,
    start, end, arrived, leaving, low, above_in, below_in,
    local, send, recv, ready,
):
    cut = lax.axis_index("cuts")
    tile = lax.axis_index("tile")
    has_up = tile > 0
    has_down = tile < tile_count - 1
    has_before = cut > 0
    has_after = cut < slices - 1
    planes, row_count, columns = x_ref.shape
    tiles = columns // LANES
    half = tiles // 2
    total_rows = row_count * tile_count
    coarse_count = row_count // 2
    last = planes - 1
    tail = OWN + row_count
    lead = SUB + SUB // 2

    pairs = [
        (x_hbm, x_ref), (fine_rows_hbm, fine_rows), (fine_weights_hbm, fine_weights),
        (coarse_rows_hbm, coarse_rows), (coarse_weights_hbm, coarse_weights),
    ]
    loads = [pltpu.make_async_copy(a, b, local.at[i]) for i, (a, b) in enumerate(pairs)]
    for load in loads:
        load.start()

    barrier = pltpu.get_barrier_semaphore()
    beside = [(has_up, cut, tile - 1), (has_down, cut, tile + 1)]

    def in_cut(there, other):
        return [
            (there, other, tile),
            (there & has_up, other, tile - 1),
            (there & has_down, other, tile + 1),
        ]

    before = in_cut(has_before, cut - 1)
    after = in_cut(has_after, cut + 1)

    def signal(semaphore, devices):
        for exists, to_cut, to_tile in devices:
            @pl.when(exists)
            def _():
                pl.semaphore_signal(
                    semaphore, inc=1, device_id=(to_cut, to_tile), device_id_type=MESH
                )

    def count(devices):
        return sum(exists.astype(jnp.int32) for exists, _, _ in devices)

    signal(barrier, beside + after)

    def remote(source, target, which, to_cut, to_tile):
        return pltpu.make_async_remote_copy(
            src_ref=source, dst_ref=target, send_sem=send.at[which], recv_sem=recv.at[which],
            device_id=(to_cut, to_tile), device_id_type=MESH,
        )

    def rows_at(row):
        return state.at[:, :, pl.ds(row, SUB), :]

    main_down = remote(rows_at(tail - SUB), rows_at(SUB), 0, cut, tile + 1)
    edge_down = remote(down_edge, from_up, 1, cut, tile + 1)
    main_up = remote(rows_at(OWN), rows_at(tail), 2, cut, tile - 1)
    edge_up = remote(up_edge, from_down, 3, cut, tile - 1)

    zero = jnp.zeros((SUB, LANES), jnp.float32)
    for j in range(tiles):
        for plane in range(planes):
            state[plane, j, pl.ds(0, SUB), :] = zero
            state[plane, j, pl.ds(tail + SUB, SUB), :] = zero
        for part in range(2):
            change[j, part, pl.ds(0, SUB), :] = zero
            change[j, part, pl.ds(tail + SUB, SUB), :] = zero
    for j in range(half):
        for row in range(0, 4 * SUB, SUB):
            for plane in range(planes):
                c_state[plane, j, pl.ds(row, SUB), :] = zero
            for part in range(2):
                c_change[j, part, pl.ds(row, SUB), :] = zero

    @pl.when(jnp.logical_not(has_up))
    def _():
        for plane in range(planes):
            for j in range(tiles):
                state[plane, j, pl.ds(SUB, SUB), :] = zero

    @pl.when(jnp.logical_not(has_down))
    def _():
        for plane in range(planes):
            for j in range(tiles):
                state[plane, j, pl.ds(tail, SUB), :] = zero

    loads[0].wait()
    for row in range(0, row_count, SUB):
        for plane in range(planes):
            values = x_ref[plane, pl.ds(row, SUB), :]
            parts = relaid([values[:, t * LANES : (t + 1) * LANES] for t in range(tiles)])
            for j in range(tiles):
                state[plane, j, pl.ds(OWN + row, SUB), :] = parts[j]
                if plane == last and row == 0:
                    down_edge[pl.ds(j, 1), :] = parts[j][SUB - 1 :]
                if plane == last and row == row_count - SUB:
                    up_edge[pl.ds(j, 1), :] = parts[j][:1]

    pl.semaphore_wait(barrier, count(beside + before))

    @pl.when(has_down)
    def _():
        main_down.start()
        edge_down.start()

    @pl.when(has_up)
    def _():
        main_up.start()
        edge_up.start()

    signal(ready, before)

    def mask(total, origin, shape):
        at = lax.broadcasted_iota(jnp.int32, shape, 0) + origin
        return ((at >= 0) & (at < total)).astype(jnp.float32)

    for load in loads[1:]:
        load.wait()
    inside = mask(total_rows, tile * row_count - SUB, (row_count + 2 * SUB, LANES))
    window = pl.ds(SUB, row_count + 2 * SUB)
    factor_in[window, :] = inside * (FINE_STEP / (2.0 * FINE_SPACING))
    for j in range(tiles):
        slope_in[j, window, :] = inside * fine_rows[3, pl.ds(j, 1), :]
        weight_in[j, window, :] = inside * fine_rows[4, pl.ds(j, 1), :]
    c_window = pl.ds(SUB, 2 * SUB)

    def restricted(plane, j, row, count):
        parts = [
            state[plane, 2 * j + k, pl.ds(row + r, count, stride=2), :]
            for r in range(2)
            for k in range(2)
        ]
        return 0.25 * ((parts[0] + parts[1]) + (parts[2] + parts[3]))

    def each_slab():
        return [(plane, j) for plane in range(planes) for j in range(half)]

    @pl.when(has_before)
    def _():
        c_inside = mask(total_rows // 2, tile * coarse_count - SUB // 2, (2 * SUB, LANES))
        c_factor_in[c_window, :] = c_inside * (COARSE_STEP / (2.0 * COARSE_SPACING))
        for j in range(half):
            c_slope_in[j, c_window, :] = c_inside * coarse_rows[3, pl.ds(j, 1), :]
            c_weight_in[j, c_window, :] = c_inside * coarse_rows[4, pl.ds(j, 1), :]

    @pl.when(has_up)
    def _():
        main_down.wait_recv()
        edge_down.wait_recv()
        for j in range(tiles):
            state[last, j, pl.ds(SUB - 1, 1), :] = from_up[pl.ds(j, 1), :]

    @pl.when(has_down)
    def _():
        main_up.wait_recv()
        edge_up.wait_recv()
        for j in range(tiles):
            state[last, j, pl.ds(tail + SUB, 1), :] = from_down[pl.ds(j, 1), :]

    @pl.when(has_before)
    def _():
        for plane, j in each_slab():
            start[plane, j] = restricted(plane, j, SUB, 2 * SUB)

    @pl.when(has_down)
    def _():
        main_down.wait_send()
        edge_down.wait_send()

    @pl.when(has_up)
    def _():
        main_up.wait_send()
        edge_up.wait_send()

    full = (SUB, row_count + 2 * SUB)
    mid = (lead, row_count + SUB)
    for wide, core in ((full, full), (full, mid), (mid, mid)):
        wave(
            state, held, change, fine_rows, fine_weights, (factor_in, slope_in, weight_in),
            tiles, tiles, wide, core,
        )

    first_part = (pl.ds(0, last), slice(None), pl.ds(0, HALO[0]))
    last_part = (last, slice(None), pl.ds(0, HALO[last]))
    to_own = remote(leaving, arrived, 4, cut + 1, tile)
    to_above = [
        remote(leaving.at[part], below_in.at[part], 5 + i, cut + 1, tile - 1)
        for i, part in enumerate((first_part, last_part))
    ]
    to_below = [
        remote(low.at[part], above_in.at[part], 7 + i, cut + 1, tile + 1)
        for i, part in enumerate((first_part, last_part))
    ]

    def leave(plane, j, value):
        leaving[plane, j] = value
        low[plane, j] = pltpu.roll(value, HALO[plane], 0)

    def launch():
        pl.semaphore_wait(ready, count(after))

        @pl.when(has_after & has_up)
        def _():
            for copy in to_above:
                copy.start()

        @pl.when(has_after & has_down)
        def _():
            for copy in to_below:
                copy.start()

        @pl.when(has_after)
        def _():
            to_own.start()

    @pl.when(cut == 0)
    def _():
        for plane, j in each_slab():
            leave(plane, j, restricted(plane, j, OWN, coarse_count))
        launch()

    for plane in range(planes):
        for row in range(0, row_count, SUB):
            parts = relaid([state[plane, j, pl.ds(OWN + row, SUB), :] for j in range(tiles)])
            for t in range(tiles):
                out_ref[plane, pl.ds(row, SUB), pl.ds(t * LANES, LANES)] = parts[t]

    @pl.when(has_before)
    def _():
        for plane, j in each_slab():
            end[plane, j] = restricted(plane, j, OWN, coarse_count)

        @pl.when(has_up)
        def _():
            for copy in to_below:
                copy.wait_recv()
            for plane, j in each_slab():
                size = HALO[plane]
                c_state[plane, j, pl.ds(lead - size, size), :] = (
                    above_in[plane, j, pl.ds(0, size), :]
                    - start[plane, j, pl.ds(SUB // 2 - size, size), :]
                )

        @pl.when(has_down)
        def _():
            for copy in to_above:
                copy.wait_recv()
            for plane, j in each_slab():
                size = HALO[plane]
                c_state[plane, j, pl.ds(lead + coarse_count, size), :] = (
                    below_in[plane, j, pl.ds(0, size), :]
                    - start[plane, j, pl.ds(SUB // 2 + coarse_count, size), :]
                )

        to_own.wait_recv()
        own = pl.ds(lead, coarse_count)
        for plane, j in each_slab():
            c_state[plane, j, own, :] = (
                arrived[plane, j] - start[plane, j, pl.ds(SUB // 2, coarse_count), :]
            )
        wave(
            c_state, c_held, c_change, coarse_rows, coarse_weights,
            (c_factor_in, c_slope_in, c_weight_in), half, tiles, (SUB, 2 * SUB), (SUB, 2 * SUB),
        )

        @pl.when(has_after)
        def _():
            for plane, j in each_slab():
                leave(plane, j, c_state[plane, j, own, :] + end[plane, j])
            launch()

        for plane in range(planes):
            parts = relaid([c_state[plane, j // 2, own, :] for j in range(tiles)])
            for t in range(tiles):
                for r in range(2):
                    spread[plane, t, pl.ds(r, coarse_count, stride=2), :] = parts[t]
            for t in range(tiles):
                at = (plane, slice(None), pl.ds(t * LANES, LANES))
                out_ref[at] = out_ref[at] + spread[plane, t]

    @pl.when(has_after & has_up)
    def _():
        for copy in to_above:
            copy.wait_send()

    @pl.when(has_after & has_down)
    def _():
        for copy in to_below:
            copy.wait_send()

    @pl.when(has_after)
    def _():
        to_own.wait_send()


def per_device(tile_count, slices, start_states):
    fields = start_states[0]
    planes, row_count, columns = fields.shape
    tiles = columns // LANES
    half = tiles // 2
    fine = line_tables(tiles, tiles, 1.0, columns, FINE_SPACING, FINE_STEP)
    coarse = line_tables(half, tiles, 2.0, columns, COARSE_SPACING, COARSE_STEP)
    fine_count = row_count + 4 * SUB
    coarse_count = row_count // 2
    c_count = coarse_count + 3 * SUB
    f32 = jnp.float32

    def vmem(*shape):
        return pltpu.VMEM(shape, f32)

    slab = vmem(planes, half, coarse_count, LANES)
    out = pl.pallas_call(
        functools.partial(kernel, tile_count, slices),
        out_shape=jax.ShapeDtypeStruct(fields.shape, f32),
        in_specs=[pl.BlockSpec(memory_space=pltpu.HBM)] * 5,
        out_specs=pl.BlockSpec(memory_space=pltpu.VMEM),
        scratch_shapes=[vmem(*fields.shape)]
        + [pltpu.VMEM(a.shape, a.dtype) for a in fine + coarse]
        + [vmem(tiles, LANES)] * 4
        + [
            vmem(planes, tiles, fine_count, LANES),
            vmem(tiles, 2 * (row_count + 2 * SUB), LANES),
            vmem(tiles, 2, fine_count, LANES),
            vmem(planes, half, c_count, LANES),
            vmem(half, 4 * SUB, LANES),
            vmem(half, 2, c_count, LANES),
            vmem(fine_count, LANES),
            vmem(tiles, fine_count, LANES),
            vmem(tiles, fine_count, LANES),
            vmem(c_count, LANES),
            vmem(half, c_count, LANES),
            vmem(half, c_count, LANES),
            vmem(planes, tiles, row_count, LANES),
            vmem(planes, half, 2 * SUB, LANES),
        ]
        + [slab] * 6
        + [
            pltpu.SemaphoreType.DMA((5,)),
            pltpu.SemaphoreType.DMA((9,)),
            pltpu.SemaphoreType.DMA((9,)),
            pltpu.SemaphoreType.REGULAR,
        ],
        compiler_params=pltpu.CompilerParams(
            collective_id=0, has_side_effects=True, vmem_limit_bytes=24 * 1024 * 1024
        ),
    )(*[pltpu.with_memory_space_constraint(jnp.asarray(a), pltpu.HBM) for a in (fields,) + fine + coarse])
    return out[None]


def solution(mesh):
    spec = P("cuts", None, "tile", None)
    body = functools.partial(per_device, mesh.shape["tile"], mesh.shape["cuts"])
    return jax.shard_map(body, mesh=mesh, in_specs=(spec,), out_specs=spec, check_vma=False)
```

time: 29.2 us -> 25.5 us (0.87)
  Pallas kernels: 29 us -> 24.3 us
  local copies, waits for them, and re-layouts: 0 us -> 0.75 us
    pallas_call x2 -> x1, Pallas kernels: 29 us -> 24.3 us  [per_device(): pl.pallas_call(functools.partial(kernel, tile_count, slices), out_shape=j...]
    unnamed x0 -> x1, local copies, waits for them, and re-layouts: none -> 0.75 us
where the time goes in v1:
time: 25.5 us; the launch traced here: 25.1 us
  Pallas kernels  24.3 us (95%)
  local copies, waits for them, and re-layouts  0.75 us (3%)
    pallas_call x1, Pallas kernels, per_device(): pl.pallas_call(functools.partial(kernel, tile_count, slices), out_shape=j...  24.3 us
    unnamed x1, local copies, waits for them, and re-layouts  0.75 us

profile of v1, /device:TPU:27, one launch (start us, length us, event | category | flops | bytes accessed | tf_op | source)
XLA Modules:
  0.0 25.1 jit_solution(17522206085061242553)
XLA Ops:
  0.0 24.3 %shard_map.55 = f32[3,16,2048]{2,1,0:T(8,128)S(1)} custom-call(f32[3,16,2048]{2,1,0:T(8,128)} %bitcast.3, f32[5,16,128]{2,1,0:T(8,128)} %constant.8.clone.fine_rows_hbm, bf16[256,256]{1,0:T(8,128)(2,1)} %constant.9.clone.fine_weights_hbm, f32[5,8,128]{2,1,0:T(8,128)} %constant.10.clone.coarse_rows_hbm, bf16[256,256]{1,0:T(8,128)(2,1)} %constant.11.clone.coarse_weights_hbm), custom_call_target="tpu_custom_call" | custom-call | tf_op jit(solution)/shard_map/pallas_call | solution.py:484
  24.3 0.7 %copy.7 = f32[1,3,16,2048]{3,2,1,0:T(8,128)} copy(f32[1,3,16,2048]{3,2,1,0:T(8,128)S(1)} %bitcast.2) | data formatting | bytes 786432

commit v2 on v1

--- a/solution.py
+++ b/solution.py
@@ -18,6 +18,7 @@
 SUB = 8
 HALO = (2, 2, 3)
 OWN = 2 * SUB
+SPILL = 5
 MESH = pl.DeviceIdType.MESH
 
 
@@ -160,10 +161,11 @@
     tile_count, slices, x_hbm, fine_rows_hbm, fine_weights_hbm, coarse_rows_hbm,
     coarse_weights_hbm, out_ref,
     x_ref, fine_rows, fine_weights, coarse_rows, coarse_weights,
-    down_edge, up_edge, from_up, from_down, state, held, change,
+    up_edge, down_edge, from_up_edge, from_down_edge, state, held, change,
+    from_up, from_down, up_spill, down_spill, from_up_spill, from_down_spill,
     c_state, c_held, c_change, factor_in, slope_in, weight_in, c_factor_in, c_slope_in,
-    c_weight_in, spread,
-    start, end, arrived, leaving, low, above_in, below_in,
+    c_weight_in, spread, start, low_start, start_above, start_below,
+    end, arrived, leaving, low, above_in, below_in,
     local, send, recv, ready,
 ):
     cut = lax.axis_index("cuts")
@@ -180,14 +182,27 @@
     last = planes - 1
     tail = OWN + row_count
     lead = SUB + SUB // 2
-
-    pairs = [
-        (x_hbm, x_ref), (fine_rows_hbm, fine_rows), (fine_weights_hbm, fine_weights),
-        (coarse_rows_hbm, coarse_rows), (coarse_weights_hbm, coarse_weights),
+    deep = HALO[last]
+
+    pairs = [(fine_rows_hbm, fine_rows)]
+    pairs += [(x_hbm.at[plane], x_ref.at[plane]) for plane in range(planes)]
+    pairs += [
+        (fine_weights_hbm, fine_weights), (coarse_rows_hbm, coarse_rows),
+        (coarse_weights_hbm, coarse_weights),
     ]
     loads = [pltpu.make_async_copy(a, b, local.at[i]) for i, (a, b) in enumerate(pairs)]
     for load in loads:
         load.start()
+
+    zero = jnp.zeros((SUB, LANES), jnp.float32)
+
+    def each_slab():
+        return [(plane, j) for plane in range(planes) for j in range(half)]
+
+    for plane, j in each_slab():
+        from_up_spill[plane, j] = zero
+        from_down_spill[plane, j, pl.ds(0, SUB), :] = zero
+        from_down_spill[plane, j, pl.ds(SUB, SUB), :] = zero
 
     barrier = pltpu.get_barrier_semaphore()
     beside = [(has_up, cut, tile - 1), (has_down, cut, tile + 1)]
@@ -221,80 +236,52 @@
             device_id=(to_cut, to_tile), device_id_type=MESH,
         )
 
-    def rows_at(row):
-        return state.at[:, :, pl.ds(row, SUB), :]
-
-    main_down = remote(rows_at(tail - SUB), rows_at(SUB), 0, cut, tile + 1)
-    edge_down = remote(down_edge, from_up, 1, cut, tile + 1)
-    main_up = remote(rows_at(OWN), rows_at(tail), 2, cut, tile - 1)
-    edge_up = remote(up_edge, from_down, 3, cut, tile - 1)
-
-    zero = jnp.zeros((SUB, LANES), jnp.float32)
+    def rows_at(ref, row, count):
+        return ref.at[:, :, pl.ds(row, count), :]
+
+    spill_up = remote(
+        rows_at(up_spill, 0, SPILL), rows_at(from_down_spill, SUB, SPILL), 0, cut, tile - 1
+    )
+    spill_down = remote(
+        rows_at(down_spill, 0, SPILL), rows_at(from_up_spill, 0, SPILL), 1, cut, tile + 1
+    )
+    rest_up = [
+        remote(rows_at(state, SUB, SUB), from_down, 2, cut, tile - 1),
+        remote(up_edge, from_down_edge, 3, cut, tile - 1),
+    ]
+    rest_down = [
+        remote(rows_at(state, tail, SUB), from_up, 4, cut, tile + 1),
+        remote(down_edge, from_up_edge, 5, cut, tile + 1),
+    ]
+    start_up = remote(rows_at(start, 0, deep), start_below, 6, cut, tile - 1)
+    start_down = remote(rows_at(low_start, 0, deep), start_above, 7, cut, tile + 1)
+
     for j in range(tiles):
-        for plane in range(planes):
-            state[plane, j, pl.ds(0, SUB), :] = zero
-            state[plane, j, pl.ds(tail + SUB, SUB), :] = zero
-        for part in range(2):
-            change[j, part, pl.ds(0, SUB), :] = zero
-            change[j, part, pl.ds(tail + SUB, SUB), :] = zero
-    for j in range(half):
-        for row in range(0, 4 * SUB, SUB):
+        for row in (0, SUB, tail, tail + SUB):
             for plane in range(planes):
-                c_state[plane, j, pl.ds(row, SUB), :] = zero
+                state[plane, j, pl.ds(row, SUB), :] = zero
             for part in range(2):
-                c_change[j, part, pl.ds(row, SUB), :] = zero
-
-    @pl.when(jnp.logical_not(has_up))
-    def _():
-        for plane in range(planes):
-            for j in range(tiles):
-                state[plane, j, pl.ds(SUB, SUB), :] = zero
-
-    @pl.when(jnp.logical_not(has_down))
-    def _():
-        for plane in range(planes):
-            for j in range(tiles):
-                state[plane, j, pl.ds(tail, SUB), :] = zero
-
-    loads[0].wait()
-    for row in range(0, row_count, SUB):
-        for plane in range(planes):
-            values = x_ref[plane, pl.ds(row, SUB), :]
-            parts = relaid([values[:, t * LANES : (t + 1) * LANES] for t in range(tiles)])
-            for j in range(tiles):
-                state[plane, j, pl.ds(OWN + row, SUB), :] = parts[j]
-                if plane == last and row == 0:
-                    down_edge[pl.ds(j, 1), :] = parts[j][SUB - 1 :]
-                if plane == last and row == row_count - SUB:
-                    up_edge[pl.ds(j, 1), :] = parts[j][:1]
-
-    pl.semaphore_wait(barrier, count(beside + before))
-
-    @pl.when(has_down)
-    def _():
-        main_down.start()
-        edge_down.start()
-
-    @pl.when(has_up)
-    def _():
-        main_up.start()
-        edge_up.start()
-
-    signal(ready, before)
+                change[j, part, pl.ds(row, SUB), :] = zero
 
     def mask(total, origin, shape):
         at = lax.broadcasted_iota(jnp.int32, shape, 0) + origin
         return ((at >= 0) & (at < total)).astype(jnp.float32)
 
-    for load in loads[1:]:
-        load.wait()
+    loads[0].wait()
     inside = mask(total_rows, tile * row_count - SUB, (row_count + 2 * SUB, LANES))
     window = pl.ds(SUB, row_count + 2 * SUB)
     factor_in[window, :] = inside * (FINE_STEP / (2.0 * FINE_SPACING))
     for j in range(tiles):
         slope_in[j, window, :] = inside * fine_rows[3, pl.ds(j, 1), :]
         weight_in[j, window, :] = inside * fine_rows[4, pl.ds(j, 1), :]
-    c_window = pl.ds(SUB, 2 * SUB)
+
+    for plane in range(planes):
+        loads[1 + plane].wait()
+        for row in range(0, row_count, SUB):
+            values = x_ref[plane, pl.ds(row, SUB), :]
+            parts = relaid([values[:, t * LANES : (t + 1) * LANES] for t in range(tiles)])
+            for j in range(tiles):
+                state[plane, j, pl.ds(OWN + row, SUB), :] = parts[j]
 
     def restricted(plane, j, row, count):
         parts = [
@@ -304,132 +291,213 @@
         ]
         return 0.25 * ((parts[0] + parts[1]) + (parts[2] + parts[3]))
 
-    def each_slab():
-        return [(plane, j) for plane in range(planes) for j in range(half)]
-
     @pl.when(has_before)
     def _():
+        for plane, j in each_slab():
+            value = restricted(plane, j, OWN, coarse_count)
+            start[plane, j] = value
+            low_start[plane, j] = pltpu.roll(value, deep, 0)
+
+    loads[1 + planes].wait()
+    inner = (lead, row_count + SUB)
+    outer = (SUB, row_count + 2 * SUB)
+    for wide, core in ((inner, inner), (inner, outer), (outer, outer)):
+        wave(
+            state, held, change, fine_rows, fine_weights, (factor_in, slope_in, weight_in),
+            tiles, tiles, wide, core,
+        )
+    for j in range(tiles):
+        for row, near, edge in ((SUB - 1, SUB, up_edge), (tail + SUB, tail + SUB - 1, down_edge)):
+            value = fine_rows[4, pl.ds(j, 1), :] * change[j, 1, pl.ds(near, 1), :]
+            state[last, j, pl.ds(row, 1), :] = value
+            edge[pl.ds(j, 1), :] = value
+
+    pl.semaphore_wait(barrier, count(beside + before))
+
+    @pl.when(has_after)
+    def _():
+        @pl.when(has_up)
+        def _():
+            for plane, j in each_slab():
+                up_spill[plane, j, pl.ds(0, SPILL), :] = restricted(
+                    plane, j, OWN - 2 * SPILL, SPILL
+                )
+            spill_up.start()
+
+        @pl.when(has_down)
+        def _():
+            for plane, j in each_slab():
+                down_spill[plane, j, pl.ds(0, SPILL), :] = restricted(plane, j, tail, SPILL)
+            spill_down.start()
+
+    @pl.when(has_before)
+    def _():
+        @pl.when(has_up)
+        def _():
+            start_up.start()
+
+        @pl.when(has_down)
+        def _():
+            start_down.start()
+
+    def pass_rest():
+        @pl.when(has_up)
+        def _():
+            for copy in rest_up:
+                copy.start()
+
+        @pl.when(has_down)
+        def _():
+            for copy in rest_down:
+                copy.start()
+
+    pl.when(has_before)(pass_rest)
+    signal(ready, before)
+    for load in loads[2 + planes :]:
+        load.wait()
+
+    first_part = (pl.ds(0, last), slice(None), pl.ds(0, HALO[0]))
+    last_part = (last, slice(None), pl.ds(0, HALO[last]))
+    to_own = remote(leaving, arrived, 8, cut + 1, tile)
+    to_above = [
+        remote(leaving.at[part], below_in.at[part], 9 + i, cut + 1, tile - 1)
+        for i, part in enumerate((first_part, last_part))
+    ]
+    to_below = [
+        remote(low.at[part], above_in.at[part], 11 + i, cut + 1, tile + 1)
+        for i, part in enumerate((first_part, last_part))
+    ]
+
+    def leave(plane, j, value):
+        leaving[plane, j] = value
+        low[plane, j] = pltpu.roll(value, HALO[plane], 0)
+
+    def launch():
+        pl.semaphore_wait(ready, count(after))
+
+        @pl.when(has_after & has_up)
+        def _():
+            for copy in to_above:
+                copy.start()
+
+        @pl.when(has_after & has_down)
+        def _():
+            for copy in to_below:
+                copy.start()
+
+        @pl.when(has_after)
+        def _():
+            to_own.start()
+
+    def landed():
+        for there, copies in (
+            (has_after & has_up, to_above), (has_after & has_down, to_below),
+            (has_after, [to_own]),
+        ):
+            @pl.when(there)
+            def _():
+                for copy in copies:
+                    copy.wait_send()
+
+    def natural():
+        for has, copies, into, edges, row, at in (
+            (has_up, rest_down, from_up, from_up_edge, OWN, OWN + SUB),
+            (has_down, rest_up, from_down, from_down_edge, tail - SUB, tail - SUB - 1),
+        ):
+            @pl.when(has)
+            def _():
+                for copy in copies:
+                    copy.wait_recv()
+                for j in range(tiles):
+                    for plane in range(planes):
+                        rows = pl.ds(row, SUB)
+                        state[plane, j, rows, :] = state[plane, j, rows, :] + into[plane, j]
+                for j in range(tiles):
+                    one = pl.ds(at, 1)
+                    state[last, j, one, :] = state[last, j, one, :] + edges[pl.ds(j, 1), :]
+
+        for plane in range(planes):
+            for row in range(0, row_count, SUB):
+                parts = relaid([state[plane, j, pl.ds(OWN + row, SUB), :] for j in range(tiles)])
+                for t in range(tiles):
+                    out_ref[plane, pl.ds(row, SUB), pl.ds(t * LANES, LANES)] = parts[t]
+
+    @pl.when(has_after)
+    def _():
+        for plane, j in each_slab():
+            end[plane, j] = restricted(plane, j, OWN, coarse_count)
+
+        @pl.when(has_up)
+        def _():
+            spill_down.wait_recv()
+
+        @pl.when(has_down)
+        def _():
+            spill_up.wait_recv()
+
+        for plane, j in each_slab():
+            value = (
+                end[plane, j]
+                + from_up_spill[plane, j]
+                + from_down_spill[plane, j, pl.ds(SPILL, SUB), :]
+            )
+            end[plane, j] = value
+
+    @pl.when(cut == 0)
+    def _():
+        for plane, j in each_slab():
+            leave(plane, j, end[plane, j])
+        launch()
+        landed()
+        pass_rest()
+
+    @pl.when(jnp.logical_not(has_after))
+    def _():
+        natural()
+
+    own = pl.ds(lead, coarse_count)
+
+    @pl.when(has_before)
+    def _():
+        c_window = pl.ds(SUB, 2 * SUB)
         c_inside = mask(total_rows // 2, tile * coarse_count - SUB // 2, (2 * SUB, LANES))
         c_factor_in[c_window, :] = c_inside * (COARSE_STEP / (2.0 * COARSE_SPACING))
         for j in range(half):
             c_slope_in[j, c_window, :] = c_inside * coarse_rows[3, pl.ds(j, 1), :]
             c_weight_in[j, c_window, :] = c_inside * coarse_rows[4, pl.ds(j, 1), :]
-
-    @pl.when(has_up)
-    def _():
-        main_down.wait_recv()
-        edge_down.wait_recv()
-        for j in range(tiles):
-            state[last, j, pl.ds(SUB - 1, 1), :] = from_up[pl.ds(j, 1), :]
-
-    @pl.when(has_down)
-    def _():
-        main_up.wait_recv()
-        edge_up.wait_recv()
-        for j in range(tiles):
-            state[last, j, pl.ds(tail + SUB, 1), :] = from_down[pl.ds(j, 1), :]
-
-    @pl.when(has_before)
-    def _():
-        for plane, j in each_slab():
-            start[plane, j] = restricted(plane, j, SUB, 2 * SUB)
-
-    @pl.when(has_down)
-    def _():
-        main_down.wait_send()
-        edge_down.wait_send()
-
-    @pl.when(has_up)
-    def _():
-        main_up.wait_send()
-        edge_up.wait_send()
-
-    full = (SUB, row_count + 2 * SUB)
-    mid = (lead, row_count + SUB)
-    for wide, core in ((full, full), (full, mid), (mid, mid)):
-        wave(
-            state, held, change, fine_rows, fine_weights, (factor_in, slope_in, weight_in),
-            tiles, tiles, wide, core,
-        )
-
-    first_part = (pl.ds(0, last), slice(None), pl.ds(0, HALO[0]))
-    last_part = (last, slice(None), pl.ds(0, HALO[last]))
-    to_own = remote(leaving, arrived, 4, cut + 1, tile)
-    to_above = [
-        remote(leaving.at[part], below_in.at[part], 5 + i, cut + 1, tile - 1)
-        for i, part in enumerate((first_part, last_part))
-    ]
-    to_below = [
-        remote(low.at[part], above_in.at[part], 7 + i, cut + 1, tile + 1)
-        for i, part in enumerate((first_part, last_part))
-    ]
-
-    def leave(plane, j, value):
-        leaving[plane, j] = value
-        low[plane, j] = pltpu.roll(value, HALO[plane], 0)
-
-    def launch():
-        pl.semaphore_wait(ready, count(after))
-
-        @pl.when(has_after & has_up)
-        def _():
-            for copy in to_above:
-                copy.start()
-
-        @pl.when(has_after & has_down)
-        def _():
-            for copy in to_below:
-                copy.start()
-
-        @pl.when(has_after)
-        def _():
-            to_own.start()
-
-    @pl.when(cut == 0)
-    def _():
-        for plane, j in each_slab():
-            leave(plane, j, restricted(plane, j, OWN, coarse_count))
-        launch()
-
-    for plane in range(planes):
-        for row in range(0, row_count, SUB):
-            parts = relaid([state[plane, j, pl.ds(OWN + row, SUB), :] for j in range(tiles)])
-            for t in range(tiles):
-                out_ref[plane, pl.ds(row, SUB), pl.ds(t * LANES, LANES)] = parts[t]
-
-    @pl.when(has_before)
-    def _():
-        for plane, j in each_slab():
-            end[plane, j] = restricted(plane, j, OWN, coarse_count)
+            for row in range(0, 4 * SUB, SUB):
+                for plane in range(planes):
+                    c_state[plane, j, pl.ds(row, SUB), :] = zero
+                for part in range(2):
+                    c_change[j, part, pl.ds(row, SUB), :] = zero
 
         @pl.when(has_up)
         def _():
+            start_down.wait_recv()
             for copy in to_below:
                 copy.wait_recv()
             for plane, j in each_slab():
                 size = HALO[plane]
                 c_state[plane, j, pl.ds(lead - size, size), :] = (
                     above_in[plane, j, pl.ds(0, size), :]
-                    - start[plane, j, pl.ds(SUB // 2 - size, size), :]
+                    - start_above[plane, j, pl.ds(deep - size, size), :]
                 )
 
         @pl.when(has_down)
         def _():
+            start_up.wait_recv()
             for copy in to_above:
                 copy.wait_recv()
             for plane, j in each_slab():
                 size = HALO[plane]
                 c_state[plane, j, pl.ds(lead + coarse_count, size), :] = (
                     below_in[plane, j, pl.ds(0, size), :]
-                    - start[plane, j, pl.ds(SUB // 2 + coarse_count, size), :]
+                    - start_below[plane, j, pl.ds(0, size), :]
                 )
 
         to_own.wait_recv()
-        own = pl.ds(lead, coarse_count)
         for plane, j in each_slab():
-            c_state[plane, j, own, :] = (
-                arrived[plane, j] - start[plane, j, pl.ds(SUB // 2, coarse_count), :]
-            )
+            c_state[plane, j, own, :] = arrived[plane, j] - start[plane, j]
         wave(
             c_state, c_held, c_change, coarse_rows, coarse_weights,
             (c_factor_in, c_slope_in, c_weight_in), half, tiles, (SUB, 2 * SUB), (SUB, 2 * SUB),
@@ -441,6 +509,12 @@
                 leave(plane, j, c_state[plane, j, own, :] + end[plane, j])
             launch()
 
+    @pl.when(has_after)
+    def _():
+        natural()
+
+    @pl.when(has_before)
+    def _():
         for plane in range(planes):
             parts = relaid([c_state[plane, j // 2, own, :] for j in range(tiles)])
             for t in range(tiles):
@@ -450,19 +524,16 @@
                 at = (plane, slice(None), pl.ds(t * LANES, LANES))
                 out_ref[at] = out_ref[at] + spread[plane, t]
 
-    @pl.when(has_after & has_up)
-    def _():
-        for copy in to_above:
-            copy.wait_send()
-
-    @pl.when(has_after & has_down)
-    def _():
-        for copy in to_below:
-            copy.wait_send()
-
-    @pl.when(has_after)
-    def _():
-        to_own.wait_send()
+    pl.when(has_before)(landed)
+    for there, copies in (
+        (has_up, rest_up), (has_down, rest_down),
+        (has_after & has_up, [spill_up]), (has_after & has_down, [spill_down]),
+        (has_before & has_up, [start_up]), (has_before & has_down, [start_down]),
+    ):
+        @pl.when(there)
+        def _():
+            for copy in copies:
+                copy.wait_send()
 
 
 def per_device(tile_count, slices, start_states):
@@ -493,6 +564,11 @@
             vmem(planes, tiles, fine_count, LANES),
             vmem(tiles, 2 * (row_count + 2 * SUB), LANES),
             vmem(tiles, 2, fine_count, LANES),
+        ]
+        + [vmem(planes, tiles, SUB, LANES)] * 2
+        + [slab] * 3
+        + [
+            vmem(planes, half, 2 * SUB, LANES),
             vmem(planes, half, c_count, LANES),
             vmem(half, 4 * SUB, LANES),
             vmem(half, 2, c_count, LANES),
@@ -503,13 +579,14 @@
             vmem(half, c_count, LANES),
             vmem(half, c_count, LANES),
             vmem(planes, tiles, row_count, LANES),
-            vmem(planes, half, 2 * SUB, LANES),
         ]
+        + [slab] * 2
+        + [vmem(planes, half, HALO[-1], LANES)] * 2
         + [slab] * 6
         + [
-            pltpu.SemaphoreType.DMA((5,)),
-            pltpu.SemaphoreType.DMA((9,)),
-            pltpu.SemaphoreType.DMA((9,)),
+            pltpu.SemaphoreType.DMA((len(fine + coarse) + planes,)),
+            pltpu.SemaphoreType.DMA((13,)),
+            pltpu.SemaphoreType.DMA((13,)),
             pltpu.SemaphoreType.REGULAR,
         ],
         compiler_params=pltpu.CompilerParams(

time: 25.5 us -> 24.2 us (0.949)
  the two profiles are of different devices: /device:TPU:27 before, /device:TPU:28 now
where the time goes in v2:
time: 24.2 us; the launch traced here: 24 us
  Pallas kernels  23.3 us (96%)
  local copies, waits for them, and re-layouts  0.75 us (3%)
    pallas_call x1, Pallas kernels, per_device(): pl.pallas_call(functools.partial(kernel, tile_count, slices), out_shape=j...  23.3 us
    unnamed x1, local copies, waits for them, and re-layouts  0.75 us

profile of v2, /device:TPU:28, one launch (start us, length us, event | category | flops | bytes accessed | tf_op | source)
XLA Modules:
  0.0 24.0 jit_solution(16271333685571859213)
XLA Ops:
  0.0 23.3 %shard_map.55 = f32[3,16,2048]{2,1,0:T(8,128)S(1)} custom-call(f32[3,16,2048]{2,1,0:T(8,128)} %bitcast.3, f32[5,16,128]{2,1,0:T(8,128)} %constant.8.clone.fine_rows_hbm, bf16[256,256]{1,0:T(8,128)(2,1)} %constant.9.clone.fine_weights_hbm, f32[5,8,128]{2,1,0:T(8,128)} %constant.10.clone.coarse_rows_hbm, bf16[256,256]{1,0:T(8,128)(2,1)} %constant.11.clone.coarse_weights_hbm), custom_call_target="tpu_custom_call" | custom-call | tf_op jit(solution)/shard_map/pallas_call | solution.py:555
  23.3 0.7 %copy.7 = f32[1,3,16,2048]{3,2,1,0:T(8,128)} copy(f32[1,3,16,2048]{3,2,1,0:T(8,128)S(1)} %bitcast.2) | data formatting | bytes 786432

commit v3 on v2

--- a/solution.py
+++ b/solution.py
@@ -19,6 +19,7 @@
 HALO = (2, 2, 3)
 OWN = 2 * SUB
 SPILL = 5
+FAR = 2 * HALO[-1]
 MESH = pl.DeviceIdType.MESH
 
 
@@ -116,45 +117,48 @@
         along = across(lambda i: state[1, i, near, :], j)
         down = state[2, j, pl.ds(h0 + 1, hn), :] - state[2, j, pl.ds(h0 - 1, hn), :]
         state[0, j, near, :] = state[0, j, near, :] - factor * (along + down)
-    total = None
-    inner = None
-    for j in range(tiles):
-        along = across(lambda i: state[0, i, at, :], j)
+    def forcing(part, j):
+        if part == 0:
+            along = across(lambda i: state[0, i, at, :], j)
+            return state[1, j, at, :] - table(3, j) * along
         down = state[0, j, pl.ds(t0 + 1, tn), :] - state[0, j, pl.ds(t0 - 1, tn), :]
-        force_x = state[1, j, at, :] - table(3, j) * along
-        force_y = state[2, j, at, :] - slope_in[j, at, :] * down
-        force = jnp.concatenate([force_x, force_y], axis=0)
-        if j == last:
-            edge = force + table(0, j) * inner
-        elif j == 0:
-            inner = force * table(0, j)
-            total = inner
-            held[j, pl.ds(0, 2 * tn), :] = inner
-        else:
-            inner = force * table(0, j) + table(1, j) * inner
-            total = total + table(2, j) * inner
-            held[j, pl.ds(0, 2 * tn), :] = inner
-    met = edge + table(0, last) * chunk_after(total)
-    high = met.astype(jnp.bfloat16)
-    low = (met - high.astype(jnp.float32)).astype(jnp.bfloat16)
-    met = jnp.dot(
-        jnp.concatenate([high, low], axis=1),
-        weights[...],
-        preferred_element_type=jnp.float32,
-    )
-    value = met[:, :LANES] + met[:, LANES:]
-    before = chunk_before(value)
-    for j in range(last, -1, -1):
-        if j < last:
-            value = (
-                held[j, pl.ds(0, 2 * tn), :] + table(2, j + 1) * before + table(1, j) * value
+        return state[2, j, at, :] - slope_in[j, at, :] * down
+
+    solved = []
+    for part in range(2):
+        spot = pl.ds(part * tn, tn)
+        total = None
+        inner = None
+        for j in range(last):
+            force = forcing(part, j)
+            if j == 0:
+                inner = force * table(0, j)
+                total = inner
+            else:
+                inner = force * table(0, j) + table(1, j) * inner
+                total = total + table(2, j) * inner
+            held[j, spot, :] = inner
+        edge = forcing(part, last) + table(0, last) * (inner + chunk_after(total))
+        high = edge.astype(jnp.bfloat16)
+        low = (edge - high.astype(jnp.float32)).astype(jnp.bfloat16)
+        solved.append(
+            jnp.dot(
+                jnp.concatenate([high, low], axis=1),
+                weights[...],
+                preferred_element_type=jnp.float32,
             )
-        for part in range(2):
-            trial = value[part * tn : (part + 1) * tn]
-            moved = trial - state[1 + part, j, at, :]
+        )
+    for part in range(2):
+        spot = pl.ds(part * tn, tn)
+        value = solved[part][:, :LANES] + solved[part][:, LANES:]
+        before = chunk_before(value)
+        for j in range(last, -1, -1):
+            if j < last:
+                value = held[j, spot, :] + table(2, j + 1) * before + table(1, j) * value
+            moved = value - state[1 + part, j, at, :]
             change[j, part, at, :] = moved
             around = change[j, part, pl.ds(t0 + 1, tn), :] + change[j, part, pl.ds(t0 - 1, tn), :]
-            state[1 + part, j, at, :] = trial + weight_in[j, at, :] * (around - 2.0 * moved)
+            state[1 + part, j, at, :] = value + weight_in[j, at, :] * (around - 2.0 * moved)
 
 
 def kernel(
@@ -164,9 +168,9 @@
     up_edge, down_edge, from_up_edge, from_down_edge, state, held, change,
     from_up, from_down, up_spill, down_spill, from_up_spill, from_down_spill,
     c_state, c_held, c_change, factor_in, slope_in, weight_in, c_factor_in, c_slope_in,
-    c_weight_in, spread, start, low_start, start_above, start_below,
-    end, arrived, leaving, low, above_in, below_in,
-    local, send, recv, ready,
+    c_weight_in, offset, spread, start, low_start, start_above, start_below,
+    end, arrived, leaving, low, above_in, below_in, far_in, far_leaving, far_low, gain,
+    far_above, far_below, side_above, side_below, local, send, recv, ready, far_ready,
 ):
     cut = lax.axis_index("cuts")
     tile = lax.axis_index("tile")
@@ -174,6 +178,10 @@
     has_down = tile < tile_count - 1
     has_before = cut > 0
     has_after = cut < slices - 1
+    odd = cut % 2 == 1
+    even = jnp.logical_not(odd)
+    has_far_before = odd & (cut > 1)
+    has_far_after = odd & (cut < slices - 2)
     planes, row_count, columns = x_ref.shape
     tiles = columns // LANES
     half = tiles // 2
@@ -216,6 +224,8 @@
 
     before = in_cut(has_before, cut - 1)
     after = in_cut(has_after, cut + 1)
+    far_before = in_cut(has_far_before, cut - 2)
+    far_after = in_cut(has_far_after, cut + 2)
 
     def signal(semaphore, devices):
         for exists, to_cut, to_tile in devices:
@@ -228,7 +238,7 @@
     def count(devices):
         return sum(exists.astype(jnp.int32) for exists, _, _ in devices)
 
-    signal(barrier, beside + after)
+    signal(barrier, beside + after + far_after)
 
     def remote(source, target, which, to_cut, to_tile):
         return pltpu.make_async_remote_copy(
@@ -312,7 +322,7 @@
             state[last, j, pl.ds(row, 1), :] = value
             edge[pl.ds(j, 1), :] = value
 
-    pl.semaphore_wait(barrier, count(beside + before))
+    pl.semaphore_wait(barrier, count(beside + before + far_before))
 
     @pl.when(has_after)
     def _():
@@ -353,6 +363,7 @@
 
     pl.when(has_before)(pass_rest)
     signal(ready, before)
+    signal(far_ready, far_before)
     for load in loads[2 + planes :]:
         load.wait()
 
@@ -368,6 +379,28 @@
         for i, part in enumerate((first_part, last_part))
     ]
 
+    far_own = remote(far_leaving, far_in, 13, cut + 2, tile)
+    far_up = remote(rows_at(far_leaving, 0, FAR), far_below, 14, cut + 2, tile - 1)
+    far_down = remote(rows_at(far_low, 0, FAR), far_above, 15, cut + 2, tile + 1)
+
+    side_up = remote(rows_at(far_leaving, 0, deep), side_below, 16, cut, tile - 1)
+    side_down = remote(rows_at(low, 0, deep), side_above, 17, cut, tile + 1)
+
+    def far_launch():
+        pl.semaphore_wait(far_ready, count(far_after))
+
+        @pl.when(has_far_after & has_up)
+        def _():
+            far_up.start()
+
+        @pl.when(has_far_after & has_down)
+        def _():
+            far_down.start()
+
+        @pl.when(has_far_after)
+        def _():
+            far_own.start()
+
     def leave(plane, j, value):
         leaving[plane, j] = value
         low[plane, j] = pltpu.roll(value, HALO[plane], 0)
@@ -375,12 +408,12 @@
     def launch():
         pl.semaphore_wait(ready, count(after))
 
-        @pl.when(has_after & has_up)
+        @pl.when(has_after & even & has_up)
         def _():
             for copy in to_above:
                 copy.start()
 
-        @pl.when(has_after & has_down)
+        @pl.when(has_after & even & has_down)
         def _():
             for copy in to_below:
                 copy.start()
@@ -391,8 +424,11 @@
 
     def landed():
         for there, copies in (
-            (has_after & has_up, to_above), (has_after & has_down, to_below),
+            (has_after & even & has_up, to_above), (has_after & even & has_down, to_below),
             (has_after, [to_own]),
+            (has_far_after & has_up, [far_up]), (has_far_after & has_down, [far_down]),
+            (has_far_after, [far_own]),
+            (odd & has_after & has_up, [side_up]), (odd & has_after & has_down, [side_down]),
         ):
             @pl.when(there)
             def _():
@@ -451,17 +487,29 @@
         landed()
         pass_rest()
 
-    @pl.when(jnp.logical_not(has_after))
-    def _():
-        natural()
-
     own = pl.ds(lead, coarse_count)
+    c_core = (SUB, 2 * SUB)
+
+    def above(size):
+        return pl.ds(lead - size, size)
+
+    def below(size):
+        return pl.ds(lead + coarse_count, size)
+
+    def coarse_wave(wide):
+        wave(
+            c_state, c_held, c_change, coarse_rows, coarse_weights,
+            (c_factor_in, c_slope_in, c_weight_in), half, tiles, wide, c_core,
+        )
 
     @pl.when(has_before)
     def _():
+        c_wide = pl.ds(SUB // 2, 3 * SUB)
         c_window = pl.ds(SUB, 2 * SUB)
-        c_inside = mask(total_rows // 2, tile * coarse_count - SUB // 2, (2 * SUB, LANES))
-        c_factor_in[c_window, :] = c_inside * (COARSE_STEP / (2.0 * COARSE_SPACING))
+        origin = tile * coarse_count - lead
+        c_inside = mask(total_rows // 2, origin + SUB // 2, (3 * SUB, LANES))
+        c_factor_in[c_wide, :] = c_inside * (COARSE_STEP / (2.0 * COARSE_SPACING))
+        c_inside = mask(total_rows // 2, origin + SUB, (2 * SUB, LANES))
         for j in range(half):
             c_slope_in[j, c_window, :] = c_inside * coarse_rows[3, pl.ds(j, 1), :]
             c_weight_in[j, c_window, :] = c_inside * coarse_rows[4, pl.ds(j, 1), :]
@@ -474,49 +522,170 @@
         @pl.when(has_up)
         def _():
             start_down.wait_recv()
+
+        @pl.when(has_down)
+        def _():
+            start_up.wait_recv()
+
+    @pl.when(has_before & even)
+    def _():
+        @pl.when(has_up)
+        def _():
+            for plane, j in each_slab():
+                c_state[plane, j, above(deep), :] = start_above[plane, j]
+
+        @pl.when(has_down)
+        def _():
+            for plane, j in each_slab():
+                c_state[plane, j, below(deep), :] = start_below[plane, j]
+
+        for plane, j in each_slab():
+            c_state[plane, j, own, :] = start[plane, j]
+        coarse_wave(c_core)
+        for plane, j in each_slab():
+            gain[plane, j] = c_state[plane, j, own, :]
+
+        @pl.when(has_after)
+        def _():
+            for plane, j in each_slab():
+                leave(plane, j, end[plane, j] - gain[plane, j])
+            launch()
+
+    @pl.when((has_before & even) | jnp.logical_not(has_after))
+    def _():
+        natural()
+
+    def joined(place):
+        @pl.when(has_up)
+        def _():
             for copy in to_below:
                 copy.wait_recv()
             for plane, j in each_slab():
                 size = HALO[plane]
-                c_state[plane, j, pl.ds(lead - size, size), :] = (
+                place(
+                    plane, j, above(size),
                     above_in[plane, j, pl.ds(0, size), :]
-                    - start_above[plane, j, pl.ds(deep - size, size), :]
+                    - start_above[plane, j, pl.ds(deep - size, size), :],
                 )
 
         @pl.when(has_down)
         def _():
-            start_up.wait_recv()
             for copy in to_above:
                 copy.wait_recv()
             for plane, j in each_slab():
                 size = HALO[plane]
-                c_state[plane, j, pl.ds(lead + coarse_count, size), :] = (
+                place(
+                    plane, j, below(size),
                     below_in[plane, j, pl.ds(0, size), :]
-                    - start_below[plane, j, pl.ds(0, size), :]
+                    - start_below[plane, j, pl.ds(0, size), :],
                 )
 
         to_own.wait_recv()
         for plane, j in each_slab():
-            c_state[plane, j, own, :] = arrived[plane, j] - start[plane, j]
-        wave(
-            c_state, c_held, c_change, coarse_rows, coarse_weights,
-            (c_factor_in, c_slope_in, c_weight_in), half, tiles, (SUB, 2 * SUB), (SUB, 2 * SUB),
-        )
+            place(plane, j, own, arrived[plane, j] - start[plane, j])
+
+    @pl.when(cut == 1)
+    def _():
+        def place(plane, j, rows, value):
+            c_state[plane, j, rows, :] = value
+
+        joined(place)
+
+    @pl.when(has_far_before)
+    def _():
+        def hold(plane, j, rows, value):
+            offset[plane, j, rows, :] = value
+
+        def add(plane, j, rows):
+            c_state[plane, j, rows, :] = c_state[plane, j, rows, :] + offset[plane, j, rows, :]
+
+        joined(hold)
+
+        @pl.when(has_up)
+        def _():
+            far_down.wait_recv()
+            for plane, j in each_slab():
+                c_state[plane, j, above(FAR), :] = far_above[plane, j]
+
+        @pl.when(has_down)
+        def _():
+            far_up.wait_recv()
+            for plane, j in each_slab():
+                c_state[plane, j, below(FAR), :] = far_below[plane, j]
+
+        far_own.wait_recv()
+        for plane, j in each_slab():
+            c_state[plane, j, own, :] = far_in[plane, j]
+        coarse_wave((SUB // 2, 3 * SUB))
+
+        @pl.when(has_up)
+        def _():
+            for plane, j in each_slab():
+                add(plane, j, above(HALO[plane]))
+
+        @pl.when(has_down)
+        def _():
+            for plane, j in each_slab():
+                add(plane, j, below(HALO[plane]))
+
+        for plane, j in each_slab():
+            add(plane, j, own)
+
+    @pl.when(odd)
+    def _():
+        coarse_wave(c_core)
+        for plane, j in each_slab():
+            gain[plane, j] = c_state[plane, j, own, :]
 
         @pl.when(has_after)
         def _():
             for plane, j in each_slab():
-                leave(plane, j, c_state[plane, j, own, :] + end[plane, j])
+                value = gain[plane, j] + end[plane, j]
+                far_leaving[plane, j] = value
+                far_low[plane, j] = pltpu.roll(value, FAR, 0)
+                low[plane, j] = pltpu.roll(value, deep, 0)
+                c_state[plane, j, own, :] = value
+            far_launch()
+
+            @pl.when(has_up)
+            def _():
+                side_up.start()
+
+            @pl.when(has_down)
+            def _():
+                side_down.start()
+
+            @pl.when(has_up)
+            def _():
+                side_down.wait_recv()
+                for plane, j in each_slab():
+                    c_state[plane, j, above(deep), :] = side_above[plane, j]
+
+            @pl.when(has_down)
+            def _():
+                side_up.wait_recv()
+                for plane, j in each_slab():
+                    c_state[plane, j, below(deep), :] = side_below[plane, j]
+
+            coarse_wave(c_core)
+            for plane, j in each_slab():
+                leaving[plane, j] = c_state[plane, j, own, :]
             launch()
 
-    @pl.when(has_after)
+    @pl.when(has_after & ((cut == 0) | odd))
     def _():
         natural()
 
+    @pl.when(has_before & even)
+    def _():
+        to_own.wait_recv()
+        for plane, j in each_slab():
+            gain[plane, j] = arrived[plane, j] - gain[plane, j]
+
     @pl.when(has_before)
     def _():
         for plane in range(planes):
-            parts = relaid([c_state[plane, j // 2, own, :] for j in range(tiles)])
+            parts = relaid([gain[plane, j // 2] for j in range(tiles)])
             for t in range(tiles):
                 for r in range(2):
                     spread[plane, t, pl.ds(r, coarse_count, stride=2), :] = parts[t]
@@ -578,15 +747,19 @@
             vmem(c_count, LANES),
             vmem(half, c_count, LANES),
             vmem(half, c_count, LANES),
+            vmem(planes, half, c_count, LANES),
             vmem(planes, tiles, row_count, LANES),
         ]
         + [slab] * 2
         + [vmem(planes, half, HALO[-1], LANES)] * 2
-        + [slab] * 6
+        + [slab] * 10
+        + [vmem(planes, half, FAR, LANES)] * 2
+        + [vmem(planes, half, HALO[-1], LANES)] * 2
         + [
             pltpu.SemaphoreType.DMA((len(fine + coarse) + planes,)),
-            pltpu.SemaphoreType.DMA((13,)),
-            pltpu.SemaphoreType.DMA((13,)),
+            pltpu.SemaphoreType.DMA((18,)),
+            pltpu.SemaphoreType.DMA((18,)),
+            pltpu.SemaphoreType.REGULAR,
             pltpu.SemaphoreType.REGULAR,
         ],
         compiler_params=pltpu.CompilerParams(

time: 24.2 us -> 23.1 us (0.955)
  the two profiles are of different devices: /device:TPU:28 before, /device:TPU:20 now
where the time goes in v3:
time: 23.1 us; the launch traced here: 23 us
  Pallas kernels  22.2 us (96%)
  local copies, waits for them, and re-layouts  0.75 us (3%)
    pallas_call x1, Pallas kernels, per_device(): pl.pallas_call(functools.partial(kernel, tile_count, slices), out_shape=j...  22.2 us
    unnamed x1, local copies, waits for them, and re-layouts  0.75 us

profile of v3, /device:TPU:20, one launch (start us, length us, event | category | flops | bytes accessed | tf_op | source)
XLA Modules:
  0.0 23.0 jit_solution(16349478199155968247)
XLA Ops:
  0.0 22.2 %shard_map.55 = f32[3,16,2048]{2,1,0:T(8,128)S(1)} custom-call(f32[3,16,2048]{2,1,0:T(8,128)} %bitcast.3, f32[5,16,128]{2,1,0:T(8,128)} %constant.8.clone.fine_rows_hbm, bf16[256,256]{1,0:T(8,128)(2,1)} %constant.9.clone.fine_weights_hbm, f32[5,8,128]{2,1,0:T(8,128)} %constant.10.clone.coarse_rows_hbm, bf16[256,256]{1,0:T(8,128)(2,1)} %constant.11.clone.coarse_weights_hbm), custom_call_target="tpu_custom_call" | custom-call | tf_op jit(solution)/shard_map/pallas_call | solution.py:724
  22.3 0.7 %copy.7 = f32[1,3,16,2048]{3,2,1,0:T(8,128)} copy(f32[1,3,16,2048]{3,2,1,0:T(8,128)S(1)} %bitcast.2) | data formatting | bytes 786432

commit v4 on v3

--- a/solution.py
+++ b/solution.py
@@ -170,7 +170,8 @@
     c_state, c_held, c_change, factor_in, slope_in, weight_in, c_factor_in, c_slope_in,
     c_weight_in, offset, spread, start, low_start, start_above, start_below,
     end, arrived, leaving, low, above_in, below_in, far_in, far_leaving, far_low, gain,
-    far_above, far_below, side_above, side_below, local, send, recv, ready, far_ready,
+    far_above, far_below, side_above, side_below, halo_up, halo_down, halo_above, halo_below,
+    local, send, recv, ready, far_ready,
 ):
     cut = lax.axis_index("cuts")
     tile = lax.axis_index("tile")
@@ -308,6 +309,9 @@
             start[plane, j] = value
             low_start[plane, j] = pltpu.roll(value, deep, 0)
 
+    pl.semaphore_wait(barrier, count(beside + before + far_before))
+    signal(ready, before)
+    signal(far_ready, far_before)
     loads[1 + planes].wait()
     inner = (lead, row_count + SUB)
     outer = (SUB, row_count + 2 * SUB)
@@ -322,8 +326,6 @@
             state[last, j, pl.ds(row, 1), :] = value
             edge[pl.ds(j, 1), :] = value
 
-    pl.semaphore_wait(barrier, count(beside + before + far_before))
-
     @pl.when(has_after)
     def _():
         @pl.when(has_up)
@@ -362,8 +364,6 @@
                 copy.start()
 
     pl.when(has_before)(pass_rest)
-    signal(ready, before)
-    signal(far_ready, far_before)
     for load in loads[2 + planes :]:
         load.wait()
 
@@ -405,7 +405,14 @@
         leaving[plane, j] = value
         low[plane, j] = pltpu.roll(value, HALO[plane], 0)
 
-    def launch():
+    first = cut == 0
+    first_own = remote(far_leaving, arrived, 8, cut + 1, tile)
+    first_halos = [
+        remote(halo_up, halo_above, 18, cut + 1, tile),
+        remote(halo_down, halo_below, 19, cut + 1, tile),
+    ]
+
+    def launch_edges():
         pl.semaphore_wait(ready, count(after))
 
         @pl.when(has_after & even & has_up)
@@ -417,6 +424,9 @@
         def _():
             for copy in to_below:
                 copy.start()
+
+    def launch():
+        launch_edges()
 
         @pl.when(has_after)
         def _():
@@ -425,7 +435,7 @@
     def landed():
         for there, copies in (
             (has_after & even & has_up, to_above), (has_after & even & has_down, to_below),
-            (has_after, [to_own]),
+            (has_before & has_after, [to_own]),
             (has_far_after & has_up, [far_up]), (has_far_after & has_down, [far_down]),
             (has_far_after, [far_own]),
             (odd & has_after & has_up, [side_up]), (odd & has_after & has_down, [side_down]),
@@ -463,6 +473,16 @@
         for plane, j in each_slab():
             end[plane, j] = restricted(plane, j, OWN, coarse_count)
 
+        @pl.when(first)
+        def _():
+            for plane, j in each_slab():
+                leave(plane, j, end[plane, j])
+                halo_up[plane, j] = restricted(plane, j, OWN - 2 * deep, deep)
+                halo_down[plane, j] = restricted(plane, j, tail, deep)
+            launch_edges()
+            for copy in first_halos:
+                copy.start()
+
         @pl.when(has_up)
         def _():
             spill_down.wait_recv()
@@ -482,8 +502,10 @@
     @pl.when(cut == 0)
     def _():
         for plane, j in each_slab():
-            leave(plane, j, end[plane, j])
-        launch()
+            far_leaving[plane, j] = end[plane, j]
+        first_own.start()
+        for copy in first_halos + [first_own]:
+            copy.wait_send()
         landed()
         pass_rest()
 
@@ -555,7 +577,7 @@
     def _():
         natural()
 
-    def joined(place):
+    def joined(place, extra_above=lambda: None, extra_below=lambda: None):
         @pl.when(has_up)
         def _():
             for copy in to_below:
@@ -567,6 +589,7 @@
                     above_in[plane, j, pl.ds(0, size), :]
                     - start_above[plane, j, pl.ds(deep - size, size), :],
                 )
+            extra_above()
 
         @pl.when(has_down)
         def _():
@@ -579,6 +602,7 @@
                     below_in[plane, j, pl.ds(0, size), :]
                     - start_below[plane, j, pl.ds(0, size), :],
                 )
+            extra_below()
 
         to_own.wait_recv()
         for plane, j in each_slab():
@@ -589,7 +613,21 @@
         def place(plane, j, rows, value):
             c_state[plane, j, rows, :] = value
 
-        joined(place)
+        def widen(rows, halo, skip):
+            for plane, j in each_slab():
+                count = HALO[plane]
+                at = rows(count)
+                c_state[plane, j, at, :] = (
+                    c_state[plane, j, at, :] + halo[plane, j, pl.ds(skip(count), count), :]
+                )
+
+        for copy in first_halos:
+            copy.wait_recv()
+        joined(place, lambda: (
+            widen(above, halo_above, lambda count: deep - count),
+        ), lambda: (
+            widen(below, halo_below, lambda count: 0),
+        ))
 
     @pl.when(has_far_before)
     def _():
@@ -754,11 +792,11 @@
         + [vmem(planes, half, HALO[-1], LANES)] * 2
         + [slab] * 10
         + [vmem(planes, half, FAR, LANES)] * 2
-        + [vmem(planes, half, HALO[-1], LANES)] * 2
+        + [vmem(planes, half, HALO[-1], LANES)] * 6
         + [
             pltpu.SemaphoreType.DMA((len(fine + coarse) + planes,)),
-            pltpu.SemaphoreType.DMA((18,)),
-            pltpu.SemaphoreType.DMA((18,)),
+            pltpu.SemaphoreType.DMA((20,)),
+            pltpu.SemaphoreType.DMA((20,)),
             pltpu.SemaphoreType.REGULAR,
             pltpu.SemaphoreType.REGULAR,
         ],

time: 23.1 us -> 22 us (0.952)
  Pallas kernels: 22.2 us -> 21.1 us
    pallas_call x1, Pallas kernels: 22.2 us -> 21.1 us  [per_device(): pl.pallas_call(functools.partial(kernel, tile_count, slices), out_shape=j...]
where the time goes in v4:
time: 22 us; the launch traced here: 21.9 us
  Pallas kernels  21.1 us (96%)
  local copies, waits for them, and re-layouts  0.75 us (3%)
    pallas_call x1, Pallas kernels, per_device(): pl.pallas_call(functools.partial(kernel, tile_count, slices), out_shape=j...  21.1 us
    unnamed x1, local copies, waits for them, and re-layouts  0.75 us

profile of v4, /device:TPU:20, one launch (start us, length us, event | category | flops | bytes accessed | tf_op | source)
XLA Modules:
  0.0 21.9 jit_solution(5701634747107680156)
XLA Ops:
  0.0 21.1 %shard_map.55 = f32[3,16,2048]{2,1,0:T(8,128)S(1)} custom-call(f32[3,16,2048]{2,1,0:T(8,128)} %bitcast.3, f32[5,16,128]{2,1,0:T(8,128)} %constant.8.clone.fine_rows_hbm, bf16[256,256]{1,0:T(8,128)(2,1)} %constant.9.clone.fine_weights_hbm, f32[5,8,128]{2,1,0:T(8,128)} %constant.10.clone.coarse_rows_hbm, bf16[256,256]{1,0:T(8,128)(2,1)} %constant.11.clone.coarse_weights_hbm), custom_call_target="tpu_custom_call" | custom-call | tf_op jit(solution)/shard_map/pallas_call | solution.py:762
  21.1 0.7 %copy.7 = f32[1,3,16,2048]{3,2,1,0:T(8,128)} copy(f32[1,3,16,2048]{3,2,1,0:T(8,128)S(1)} %bitcast.2) | data formatting | bytes 786432

commit v5 on v4

--- a/solution.py
+++ b/solution.py
@@ -169,7 +169,7 @@
     from_up, from_down, up_spill, down_spill, from_up_spill, from_down_spill,
     c_state, c_held, c_change, factor_in, slope_in, weight_in, c_factor_in, c_slope_in,
     c_weight_in, offset, spread, start, low_start, start_above, start_below,
-    end, arrived, leaving, low, above_in, below_in, far_in, far_leaving, far_low, gain,
+    end, arrived, leaving, low, above_in, below_in, far_in, far_leaving, far_low, near_low, gain,
     far_above, far_below, side_above, side_below, halo_up, halo_down, halo_above, halo_below,
     local, send, recv, ready, far_ready,
 ):
@@ -213,6 +213,11 @@
         from_down_spill[plane, j, pl.ds(0, SUB), :] = zero
         from_down_spill[plane, j, pl.ds(SUB, SUB), :] = zero
 
+    right = tile % 2 == 1
+    left = jnp.logical_not(right)
+    pair_up, pair_down = has_up & right, has_down & left
+    cross_up, cross_down = has_up & left, has_down & right
+
     barrier = pltpu.get_barrier_semaphore()
     beside = [(has_up, cut, tile - 1), (has_down, cut, tile + 1)]
 
@@ -383,17 +388,19 @@
     far_up = remote(rows_at(far_leaving, 0, FAR), far_below, 14, cut + 2, tile - 1)
     far_down = remote(rows_at(far_low, 0, FAR), far_above, 15, cut + 2, tile + 1)
 
+    near_up = remote(rows_at(far_in, 0, FAR), far_below, 20, cut, tile - 1)
+    near_down = remote(rows_at(near_low, 0, FAR), far_above, 21, cut, tile + 1)
     side_up = remote(rows_at(far_leaving, 0, deep), side_below, 16, cut, tile - 1)
     side_down = remote(rows_at(low, 0, deep), side_above, 17, cut, tile + 1)
 
     def far_launch():
         pl.semaphore_wait(far_ready, count(far_after))
 
-        @pl.when(has_far_after & has_up)
+        @pl.when(has_far_after & cross_up)
         def _():
             far_up.start()
 
-        @pl.when(has_far_after & has_down)
+        @pl.when(has_far_after & cross_down)
         def _():
             far_down.start()
 
@@ -436,7 +443,8 @@
         for there, copies in (
             (has_after & even & has_up, to_above), (has_after & even & has_down, to_below),
             (has_before & has_after, [to_own]),
-            (has_far_after & has_up, [far_up]), (has_far_after & has_down, [far_down]),
+            (has_far_after & cross_up, [far_up]), (has_far_after & cross_down, [far_down]),
+            (has_far_before & pair_up, [near_up]), (has_far_before & pair_down, [near_down]),
             (has_far_after, [far_own]),
             (odd & has_after & has_up, [side_up]), (odd & has_after & has_down, [side_down]),
         ):
@@ -638,22 +646,47 @@
             c_state[plane, j, rows, :] = c_state[plane, j, rows, :] + offset[plane, j, rows, :]
 
         joined(hold)
+        far_own.wait_recv()
+
+        @pl.when(pair_up)
+        def _():
+            near_up.start()
+
+        @pl.when(pair_down)
+        def _():
+            for plane, j in each_slab():
+                near_low[plane, j] = pltpu.roll(far_in[plane, j], FAR, 0)
+            near_down.start()
+
+        for plane, j in each_slab():
+            c_state[plane, j, own, :] = far_in[plane, j]
+
+        @pl.when(cross_up)
+        def _():
+            far_down.wait_recv()
+
+        @pl.when(cross_down)
+        def _():
+            far_up.wait_recv()
+
+        @pl.when(pair_up)
+        def _():
+            near_down.wait_recv()
+
+        @pl.when(pair_down)
+        def _():
+            near_up.wait_recv()
 
         @pl.when(has_up)
         def _():
-            far_down.wait_recv()
             for plane, j in each_slab():
                 c_state[plane, j, above(FAR), :] = far_above[plane, j]
 
         @pl.when(has_down)
         def _():
-            far_up.wait_recv()
             for plane, j in each_slab():
                 c_state[plane, j, below(FAR), :] = far_below[plane, j]
 
-        far_own.wait_recv()
-        for plane, j in each_slab():
-            c_state[plane, j, own, :] = far_in[plane, j]
         coarse_wave((SUB // 2, 3 * SUB))
 
         @pl.when(has_up)
@@ -790,13 +823,13 @@
         ]
         + [slab] * 2
         + [vmem(planes, half, HALO[-1], LANES)] * 2
-        + [slab] * 10
+        + [slab] * 11
         + [vmem(planes, half, FAR, LANES)] * 2
         + [vmem(planes, half, HALO[-1], LANES)] * 6
         + [
             pltpu.SemaphoreType.DMA((len(fine + coarse) + planes,)),
-            pltpu.SemaphoreType.DMA((20,)),
-            pltpu.SemaphoreType.DMA((20,)),
+            pltpu.SemaphoreType.DMA((22,)),
+            pltpu.SemaphoreType.DMA((22,)),
             pltpu.SemaphoreType.REGULAR,
             pltpu.SemaphoreType.REGULAR,
         ],

time: 22 us -> 21.3 us (0.968)
  the two profiles are of different devices: /device:TPU:20 before, /device:TPU:29 now
where the time goes in v5:
time: 21.3 us; the launch traced here: 21.2 us
  Pallas kernels  20.4 us (96%)
  local copies, waits for them, and re-layouts  0.75 us (4%)
    pallas_call x1, Pallas kernels, per_device(): pl.pallas_call(functools.partial(kernel, tile_count, slices), out_shape=j...  20.4 us
    unnamed x1, local copies, waits for them, and re-layouts  0.75 us

profile of v5, /device:TPU:29, one launch (start us, length us, event | category | flops | bytes accessed | tf_op | source)
XLA Modules:
  0.0 21.2 jit_solution(12491121581098275857)
XLA Ops:
  0.0 20.4 %shard_map.55 = f32[3,16,2048]{2,1,0:T(8,128)S(1)} custom-call(f32[3,16,2048]{2,1,0:T(8,128)} %bitcast.3, f32[5,16,128]{2,1,0:T(8,128)} %constant.8.clone.fine_rows_hbm, bf16[256,256]{1,0:T(8,128)(2,1)} %constant.9.clone.fine_weights_hbm, f32[5,8,128]{2,1,0:T(8,128)} %constant.10.clone.coarse_rows_hbm, bf16[256,256]{1,0:T(8,128)(2,1)} %constant.11.clone.coarse_weights_hbm), custom_call_target="tpu_custom_call" | custom-call | tf_op jit(solution)/shard_map/pallas_call | solution.py:795
  20.4 0.7 %copy.7 = f32[1,3,16,2048]{3,2,1,0:T(8,128)} copy(f32[1,3,16,2048]{3,2,1,0:T(8,128)S(1)} %bitcast.2) | data formatting | bytes 786432

commit v6 on v5

--- a/solution.py
+++ b/solution.py
@@ -394,8 +394,6 @@
     side_down = remote(rows_at(low, 0, deep), side_above, 17, cut, tile + 1)
 
     def far_launch():
-        pl.semaphore_wait(far_ready, count(far_after))
-
         @pl.when(has_far_after & cross_up)
         def _():
             far_up.start()
@@ -403,10 +401,6 @@
         @pl.when(has_far_after & cross_down)
         def _():
             far_down.start()
-
-        @pl.when(has_far_after)
-        def _():
-            far_own.start()
 
     def leave(plane, j, value):
         leaving[plane, j] = value
@@ -506,11 +500,10 @@
                 + from_down_spill[plane, j, pl.ds(SPILL, SUB), :]
             )
             end[plane, j] = value
+            far_leaving[plane, j] = value
 
     @pl.when(cut == 0)
     def _():
-        for plane, j in each_slab():
-            far_leaving[plane, j] = end[plane, j]
         first_own.start()
         for copy in first_halos + [first_own]:
             copy.wait_send()
@@ -705,16 +698,27 @@
     @pl.when(odd)
     def _():
         coarse_wave(c_core)
-        for plane, j in each_slab():
-            gain[plane, j] = c_state[plane, j, own, :]
+
+        @pl.when(jnp.logical_not(has_after))
+        def _():
+            for plane, j in each_slab():
+                gain[plane, j] = c_state[plane, j, own, :]
 
         @pl.when(has_after)
         def _():
             for plane, j in each_slab():
-                value = gain[plane, j] + end[plane, j]
-                far_leaving[plane, j] = value
+                far_leaving[plane, j] = c_state[plane, j, own, :] + end[plane, j]
+            pl.semaphore_wait(far_ready, count(far_after))
+
+            @pl.when(has_far_after)
+            def _():
+                far_own.start()
+
+            for plane, j in each_slab():
+                value = far_leaving[plane, j]
                 far_low[plane, j] = pltpu.roll(value, FAR, 0)
                 low[plane, j] = pltpu.roll(value, deep, 0)
+                gain[plane, j] = c_state[plane, j, own, :]
                 c_state[plane, j, own, :] = value
             far_launch()
 

time: 21.3 us -> 21.1 us (level)
  no operation moved by 1% of the time
where the time goes in v6:
time: 21.1 us; the launch traced here: 21 us
  Pallas kernels  20.2 us (96%)
  local copies, waits for them, and re-layouts  0.75 us (4%)
    pallas_call x1, Pallas kernels, per_device(): pl.pallas_call(functools.partial(kernel, tile_count, slices), out_shape=j...  20.2 us
    unnamed x1, local copies, waits for them, and re-layouts  0.75 us

profile of v6, /device:TPU:29, one launch (start us, length us, event | category | flops | bytes accessed | tf_op | source)
XLA Modules:
  0.0 21.0 jit_solution(6041323685757911016)
XLA Ops:
  0.0 20.2 %shard_map.55 = f32[3,16,2048]{2,1,0:T(8,128)S(1)} custom-call(f32[3,16,2048]{2,1,0:T(8,128)} %bitcast.3, f32[5,16,128]{2,1,0:T(8,128)} %constant.8.clone.fine_rows_hbm, bf16[256,256]{1,0:T(8,128)(2,1)} %constant.9.clone.fine_weights_hbm, f32[5,8,128]{2,1,0:T(8,128)} %constant.10.clone.coarse_rows_hbm, bf16[256,256]{1,0:T(8,128)(2,1)} %constant.11.clone.coarse_weights_hbm), custom_call_target="tpu_custom_call" | custom-call | tf_op jit(solution)/shard_map/pallas_call | solution.py:799
  20.3 0.7 %copy.7 = f32[1,3,16,2048]{3,2,1,0:T(8,128)} copy(f32[1,3,16,2048]{3,2,1,0:T(8,128)S(1)} %bitcast.2) | data formatting | bytes 786432

commit v7 on v6

--- a/solution.py
+++ b/solution.py
@@ -333,19 +333,22 @@
 
     @pl.when(has_after)
     def _():
-        @pl.when(has_up)
-        def _():
+        def spill_to_up():
             for plane, j in each_slab():
                 up_spill[plane, j, pl.ds(0, SPILL), :] = restricted(
                     plane, j, OWN - 2 * SPILL, SPILL
                 )
             spill_up.start()
 
-        @pl.when(has_down)
-        def _():
+        def spill_to_down():
             for plane, j in each_slab():
                 down_spill[plane, j, pl.ds(0, SPILL), :] = restricted(plane, j, tail, SPILL)
             spill_down.start()
+
+        pl.when(cross_up)(spill_to_up)
+        pl.when(cross_down)(spill_to_down)
+        pl.when(pair_up)(spill_to_up)
+        pl.when(pair_down)(spill_to_down)
 
     @pl.when(has_before)
     def _():

time: 21.1 us -> 20.9 us (level)
  the two profiles are of different devices: /device:TPU:29 before, /device:TPU:27 now
where the time goes in v7:
time: 20.9 us; the launch traced here: 20.6 us
  Pallas kernels  19.8 us (95%)
  local copies, waits for them, and re-layouts  0.75 us (4%)
    pallas_call x1, Pallas kernels, per_device(): pl.pallas_call(functools.partial(kernel, tile_count, slices), out_shape=j...  19.8 us
    unnamed x1, local copies, waits for them, and re-layouts  0.75 us

profile of v7, /device:TPU:27, one launch (start us, length us, event | category | flops | bytes accessed | tf_op | source)
XLA Modules:
  0.0 20.6 jit_solution(11313588462924614144)
XLA Ops:
  0.0 19.8 %shard_map.55 = f32[3,16,2048]{2,1,0:T(8,128)S(1)} custom-call(f32[3,16,2048]{2,1,0:T(8,128)} %bitcast.3, f32[5,16,128]{2,1,0:T(8,128)} %constant.8.clone.fine_rows_hbm, bf16[256,256]{1,0:T(8,128)(2,1)} %constant.9.clone.fine_weights_hbm, f32[5,8,128]{2,1,0:T(8,128)} %constant.10.clone.coarse_rows_hbm, bf16[256,256]{1,0:T(8,128)(2,1)} %constant.11.clone.coarse_weights_hbm), custom_call_target="tpu_custom_call" | custom-call | tf_op jit(solution)/shard_map/pallas_call | solution.py:802
  19.8 0.7 %copy.7 = f32[1,3,16,2048]{3,2,1,0:T(8,128)} copy(f32[1,3,16,2048]{3,2,1,0:T(8,128)S(1)} %bitcast.2) | data formatting | bytes 786432

commit v8 on v7

--- a/solution.py
+++ b/solution.py
@@ -317,6 +317,17 @@
     pl.semaphore_wait(barrier, count(beside + before + far_before))
     signal(ready, before)
     signal(far_ready, far_before)
+
+    @pl.when(has_before)
+    def _():
+        @pl.when(has_up)
+        def _():
+            start_up.start()
+
+        @pl.when(has_down)
+        def _():
+            start_down.start()
+
     loads[1 + planes].wait()
     inner = (lead, row_count + SUB)
     outer = (SUB, row_count + 2 * SUB)
@@ -350,16 +361,6 @@
         pl.when(pair_up)(spill_to_up)
         pl.when(pair_down)(spill_to_down)
 
-    @pl.when(has_before)
-    def _():
-        @pl.when(has_up)
-        def _():
-            start_up.start()
-
-        @pl.when(has_down)
-        def _():
-            start_down.start()
-
     def pass_rest():
         @pl.when(has_up)
         def _():
@@ -371,7 +372,7 @@
             for copy in rest_down:
                 copy.start()
 
-    pl.when(has_before)(pass_rest)
+    pl.when(jnp.logical_not(has_after))(pass_rest)
     for load in loads[2 + planes :]:
         load.wait()
 
@@ -505,6 +506,8 @@
             end[plane, j] = value
             far_leaving[plane, j] = value
 
+    pl.when(has_before & has_after)(pass_rest)
+
     @pl.when(cut == 0)
     def _():
         first_own.start()
@@ -725,13 +728,11 @@
                 c_state[plane, j, own, :] = value
             far_launch()
 
-            @pl.when(has_up)
-            def _():
-                side_up.start()
-
-            @pl.when(has_down)
-            def _():
-                side_down.start()
+            for there, copy in (
+                (cross_up, side_up), (cross_down, side_down),
+                (pair_up, side_up), (pair_down, side_down),
+            ):
+                pl.when(there)(copy.start)
 
             @pl.when(has_up)
             def _():

time: 20.9 us -> 20.7 us (level)
  no operation moved by 1% of the time
where the time goes in v8:
time: 20.7 us; the launch traced here: 20.5 us
  Pallas kernels  19.8 us (96%)
  local copies, waits for them, and re-layouts  0.75 us (4%)
    pallas_call x1, Pallas kernels, per_device(): pl.pallas_call(functools.partial(kernel, tile_count, slices), out_shape=j...  19.8 us
    unnamed x1, local copies, waits for them, and re-layouts  0.75 us

profile of v8, /device:TPU:27, one launch (start us, length us, event | category | flops | bytes accessed | tf_op | source)
XLA Modules:
  0.0 20.5 jit_solution(2927488409978739292)
XLA Ops:
  0.0 19.8 %shard_map.55 = f32[3,16,2048]{2,1,0:T(8,128)S(1)} custom-call(f32[3,16,2048]{2,1,0:T(8,128)} %bitcast.3, f32[5,16,128]{2,1,0:T(8,128)} %constant.8.clone.fine_rows_hbm, bf16[256,256]{1,0:T(8,128)(2,1)} %constant.9.clone.fine_weights_hbm, f32[5,8,128]{2,1,0:T(8,128)} %constant.10.clone.coarse_rows_hbm, bf16[256,256]{1,0:T(8,128)(2,1)} %constant.11.clone.coarse_weights_hbm), custom_call_target="tpu_custom_call" | custom-call | tf_op jit(solution)/shard_map/pallas_call | solution.py:803
  19.8 0.7 %copy.7 = f32[1,3,16,2048]{3,2,1,0:T(8,128)} copy(f32[1,3,16,2048]{3,2,1,0:T(8,128)S(1)} %bitcast.2) | data formatting | bytes 786432

commit v9 on v8

--- a/solution.py
+++ b/solution.py
@@ -705,11 +705,6 @@
     def _():
         coarse_wave(c_core)
 
-        @pl.when(jnp.logical_not(has_after))
-        def _():
-            for plane, j in each_slab():
-                gain[plane, j] = c_state[plane, j, own, :]
-
         @pl.when(has_after)
         def _():
             for plane, j in each_slab():
@@ -761,16 +756,25 @@
         for plane, j in each_slab():
             gain[plane, j] = arrived[plane, j] - gain[plane, j]
 
-    @pl.when(has_before)
-    def _():
+    def deliver(load):
         for plane in range(planes):
-            parts = relaid([gain[plane, j // 2] for j in range(tiles)])
+            parts = relaid([load(plane, j // 2) for j in range(tiles)])
             for t in range(tiles):
                 for r in range(2):
                     spread[plane, t, pl.ds(r, coarse_count, stride=2), :] = parts[t]
             for t in range(tiles):
                 at = (plane, slice(None), pl.ds(t * LANES, LANES))
                 out_ref[at] = out_ref[at] + spread[plane, t]
+
+    straight = odd & jnp.logical_not(has_after)
+
+    @pl.when(straight)
+    def _():
+        deliver(lambda plane, j: c_state[plane, j, own, :])
+
+    @pl.when(has_before & jnp.logical_not(straight))
+    def _():
+        deliver(lambda plane, j: gain[plane, j])
 
     pl.when(has_before)(landed)
     for there, copies in (

time: 20.7 us -> 20.7 us (level)
  no operation moved by 1% of the time
where the time goes in v9:
time: 20.7 us; the launch traced here: 20.6 us
  Pallas kernels  19.8 us (96%)
  local copies, waits for them, and re-layouts  0.75 us (4%)
    pallas_call x1, Pallas kernels, per_device(): pl.pallas_call(functools.partial(kernel, tile_count, slices), out_shape=j...  19.8 us
    unnamed x1, local copies, waits for them, and re-layouts  0.75 us

profile of v9, /device:TPU:27, one launch (start us, length us, event | category | flops | bytes accessed | tf_op | source)
XLA Modules:
  0.0 20.6 jit_solution(18363650692236989133)
XLA Ops:
  0.0 19.8 %shard_map.55 = f32[3,16,2048]{2,1,0:T(8,128)S(1)} custom-call(f32[3,16,2048]{2,1,0:T(8,128)} %bitcast.3, f32[5,16,128]{2,1,0:T(8,128)} %constant.8.clone.fine_rows_hbm, bf16[256,256]{1,0:T(8,128)(2,1)} %constant.9.clone.fine_weights_hbm, f32[5,8,128]{2,1,0:T(8,128)} %constant.10.clone.coarse_rows_hbm, bf16[256,256]{1,0:T(8,128)(2,1)} %constant.11.clone.coarse_weights_hbm), custom_call_target="tpu_custom_call" | custom-call | tf_op jit(solution)/shard_map/pallas_call | solution.py:807
  19.8 0.7 %copy.7 = f32[1,3,16,2048]{3,2,1,0:T(8,128)} copy(f32[1,3,16,2048]{3,2,1,0:T(8,128)S(1)} %bitcast.2) | data formatting | bytes 786432
